TPU v7x, 256 devices: a whole 4x4x8 slice. The times are simulated.
256 devices in a mesh: chan: 32 (over z_lo, x, core), inp: 8 (over z_hi, y).
Axes of the slice: x: 4, y: 4, z: 8 (z_hi: 2, z_lo: 4; z = z_hi * 4 + z_lo), core: 2. Of those that a mesh axis runs over, the one named last changes fastest.
Arguments:
- voltages: bfloat16 [512, 2, 131072], P('inp', None, 'chan'), may hold values from -64 to 64
Outputs:
- delays: float32 [512, 512, 2, 512], P('inp', 'chan')
All inputs are finite; a program needn't handle non-finite values.
Results may differ from a plain program's by a relative error of at most 0.0053.
Values may be sent and summed in bfloat16 or wider, within the bound.
No kernel may reach another device: no remote copies, remote signals or barrier semaphores. Data moves between devices by JAX's collectives and lax.ppermute only.
A program may use at most 128 MiB of HBM per device.

v0:
```python
import math

import jax
import jax.numpy as jnp
from jax import lax
from jax.sharding import PartitionSpec as P

NCH = 512


def taper_weights(count):
    position = jnp.arange(count, dtype=jnp.float32)
    return 0.5 - 0.5 * jnp.cos(2.0 * math.pi * (position + 0.5) / count)


def channel_table(count):
    indices = jnp.arange(count, dtype=jnp.int32)
    product = indices[:, None] * indices[None, :] % count
    angle = 2.0 * math.pi / count * product.astype(jnp.float32)
    window = taper_weights(count)[:, None] / math.sqrt(count)
    cosine = window * jnp.cos(angle)
    sine = window * jnp.sin(angle)
    upper = jnp.concatenate([cosine, -sine], axis=1)
    lower = jnp.concatenate([sine, cosine], axis=1)
    return jnp.concatenate([upper, lower], axis=0).astype(jnp.bfloat16)


def dft_tables(row_count, col_count, modulus):
    row_idx = jnp.arange(row_count, dtype=jnp.int32)
    col_idx = jnp.arange(col_count, dtype=jnp.int32)
    angle = (
        2.0
        * math.pi
        / modulus
        * (row_idx[:, None] * col_idx[None, :] % modulus).astype(jnp.float32)
    )
    return (jnp.cos(angle), jnp.sin(angle))


def complex_section(real_in, imag_in, cosine, sine, form):
    highest = lax.Precision.HIGHEST
    real_out = jnp.einsum(form, cosine, real_in, precision=highest) + jnp.einsum(
        form, sine, imag_in, precision=highest
    )
    imag_out = jnp.einsum(form, cosine, imag_in, precision=highest) - jnp.einsum(
        form, sine, real_in, precision=highest
    )
    return (real_out, imag_out)


def rotate(real_in, imag_in, cosine, sine):
    return (real_in * cosine + imag_in * sine, imag_in * cosine - real_in * sine)


def shards(voltages):
    input_rows = voltages.shape[0]
    local_time = voltages.shape[2]
    chan_count = lax.axis_size("chan")
    spec_local = local_time // NCH
    chan_local = NCH // chan_count
    table = channel_table(NCH)
    table = (
        table.reshape(2 * NCH, 2, chan_local, chan_count)
        .transpose(0, 1, 3, 2)
        .reshape(2 * NCH, 2 * NCH)
    )
    samples = (
        voltages.reshape(input_rows, 2, spec_local, NCH)
        .transpose(0, 2, 1, 3)
        .reshape(input_rows * spec_local, 2 * NCH)
    )
    spectra = jnp.dot(samples, table, preferred_element_type=jnp.float32).astype(jnp.bfloat16)
    spectra = spectra.reshape(input_rows, spec_local, 2, NCH)
    turned = lax.all_to_all(spectra, "chan", split_axis=3, concat_axis=1, tiled=True)
    spec_total = turned.shape[1]
    mine = turned.transpose(3, 0, 2, 1).reshape(chan_local, input_rows, 2 * spec_total)
    own_power = jnp.sum(jnp.square(mine.astype(jnp.float32)), axis=2) / spec_total + 1e-06
    own_scale = lax.rsqrt(own_power)
    piece = lax.all_gather(mine, "inp", axis=1, tiled=True)
    half = piece.shape[2] // 2
    rotated = jnp.concatenate([-piece[:, :, half:], piece[:, :, :half]], axis=2)
    numbers = (((2,), (2,)), ((0,), (0,)))
    real_part = lax.dot_general(mine, piece, numbers, preferred_element_type=jnp.float32)
    imag_part = lax.dot_general(mine, rotated, numbers, preferred_element_type=jnp.float32)
    power = jnp.sum(jnp.square(piece.astype(jnp.float32)), axis=2) / spec_total + 1e-06
    scaling = own_scale[:, :, None] * lax.rsqrt(power)[:, None, :] / spec_total
    rho = jnp.stack([real_part * scaling, imag_part * scaling], axis=1).astype(jnp.bfloat16)
    col_local = rho.shape[3] // chan_count
    baseline_count = input_rows * col_local
    chan_index = lax.axis_index("chan")
    position = (chan_count * jnp.arange(chan_local, dtype=jnp.int32) + chan_index).astype(
        jnp.float32
    )
    taper_local = 0.5 - 0.5 * jnp.cos(2.0 * math.pi * (position + 0.5) / NCH)
    weighted = rho.astype(jnp.float32) * taper_local[:, None, None, None]
    cos_first, sin_first = dft_tables(chan_local, chan_local, chan_local)
    section_real, section_imag = complex_section(
        weighted[:, 0], weighted[:, 1], cos_first, sin_first, "ka,aij->kij"
    )
    twist = (
        2.0
        * math.pi
        / NCH
        * (chan_index * jnp.arange(chan_local, dtype=jnp.int32) % NCH).astype(jnp.float32)
    )
    section_real, section_imag = rotate(
        section_real, section_imag, jnp.cos(twist)[:, None, None], jnp.sin(twist)[:, None, None]
    )
    paired = jnp.stack([section_real, section_imag], axis=1)
    arranged = paired.reshape(chan_local, 2, input_rows, chan_count, col_local).transpose(
        3, 0, 1, 2, 4
    )
    arranged = arranged.reshape(chan_count, chan_local, 2, baseline_count)
    regrouped = lax.all_to_all(arranged, "chan", split_axis=0, concat_axis=0, tiled=True)
    cos_second, sin_second = dft_tables(chan_count, chan_count, chan_count)
    out_real, out_imag = complex_section(
        regrouped[:, :, 0], regrouped[:, :, 1], cos_second, sin_second, "mb,bkn->mkn"
    )
    factor = math.sqrt(spec_total / NCH)
    combined = (
        jnp.stack(
            [out_real.reshape(NCH, baseline_count), out_imag.reshape(NCH, baseline_count)], axis=0
        )
        * factor
    )
    result = combined.transpose(2, 0, 1).reshape(input_rows, col_local, 2, NCH)
    rows_global = lax.axis_index("inp") * input_rows + jnp.arange(input_rows, dtype=jnp.int32)
    cols_global = lax.axis_index("chan") * col_local + jnp.arange(col_local, dtype=jnp.int32)
    same = rows_global[:, None] == cols_global[None, :]
    return jnp.where(same[:, :, None, None], jnp.zeros_like(result), result)


def solution(mesh):
    in_specs = (P("inp", None, "chan"),)
    out_specs = P("inp", "chan", None, None)
    return jax.shard_map(shards, mesh=mesh, in_specs=in_specs, out_specs=out_specs, check_vma=False)
```

profile of v0, /device:TPU:1, one launch (start us, length us, event | category | flops | bytes accessed | tf_op | source)
XLA Modules:
  0.0 456.4 jit_solution(16119081496924792960)
XLA Ops:
  6.5 0.0 all-gather.2.cloned.1.call-start
  6.6 1.8 reshape.197
  8.4 4.7 %negate_convert_fusion = (bf16[512,1,16,32]{0,2,3,1:T(8,128)(2,1)S(1)}, bf16[512,1,16,32]{0,2,3,1:T(8,128)(2,1)S(1)}, bf16[512,1,16,32]{0,2,3,1:T(8,128)(2,1)S(1)}) fusion(s32[16,32]{0,1:T(8,128)S(1)} %multiply_add_fusion.1, f32[512]{0:T(512)S(1)} %subtract_multiply_fusion), kind=kLoop, calls=%fused_computation.48 | loop fusion | flops 5242880 | bytes 1576960 | tf_op jit(solution)/shard_map/convert.9
  13.1 0.3 maximum_maximum_fusion
  13.4 1.3 fusion.28
  14.7 0.5 copy.57
  15.2 0.8 reshape.199
  16.0 2.9 copy.58
  18.9 1.5 reshape.207
  20.4 36.5 %all_to_all.23 = bf16[32,2,8192]{2,1,0:T(2,128)(2,1)S(1)} all-to-all(bf16[32,2,8192]{2,1,0:T(2,128)(2,1)S(1)} %reshape.207), channel_id=1, replica_groups=mesh['chan'=32,'inp'=8] {'chan'}, dimensions={0} | all-to-all | bytes 2097152 | tf_op jit(solution)/shard_map/all_to_all | solution.py:74
  56.8 2.3 reshape.208
  59.1 2.1 copy.60
  61.3 2.7 copy.61
  64.0 1.5 reshape.200
  65.5 0.0 all-gather.2.cloned.1.call-update
  65.6 0.1 fusion.74
  65.6 0.7 multiply_reduce_fusion.1
  66.4 170.8 %all-gather.2.cloned.1.call-done = bf16[16,512,512]{2,1,0:T(8,128)(2,1)} async-done(((bf16[16,64,512]{2,1,0:T(8,128)(2,1)}), bf16[16,512,512]{2,1,0:T(8,128)(2,1)}) %all-gather.2.cloned.1.call-update) | async-done | bytes 8388624 | tf_op jit(solution)/shard_map/all_gather | solution.py:79
  237.1 0.0 copy-start
  237.1 5.3 %multiply_reduce_fusion = f32[16,512]{1,0:T(8,128)S(1)} fusion(bf16[16,512,512]{2,1,0:T(8,128)(2,1)} %all-gather.2.cloned.1.call-done), kind=kLoop, calls=%fused_computation | loop fusion | flops 12574720 | bytes 8421376 | tf_op jit(solution)/shard_map/reduce_sum | solution.py:85
  242.4 0.5 copy-done
  242.9 0.0 copy-start.1
  242.9 0.6 slice_negate_fusion
  243.5 0.6 copy-done.1
  244.1 3.0 fusion.29
  247.2 2.6 fusion.27
  249.8 0.7 convert_multiply_fusion
  250.5 0.7 slice_bitcast_fusion.1
  251.2 2.9 fusion.11
  254.1 2.9 fusion.9
  257.0 2.9 fusion.17
  259.9 17.3 %multiply_add_fusion = (f32[16,64,512]{2,0,1:T(8,128)}, f32[16,64,512]{2,0,1:T(8,128)S(1)}) fusion(f32[16,64,512]{2,0,1:T(8,128)S(1)} %fusion.17, f32[16]{0:T(128)S(1)} %get-tuple-element.16, f32[16]{0:T(128)S(1)} %get-tuple-element.17, f32[16,64,512]{2,0,1:T(8,128)S(1)} %fusion.9, f32[16,64,512]{2,1,0:T(8,128)S(1)} %get-tuple-element.11), kind=kOutput, calls=%fused_computation.17 | convolution fusion | flops 104336896 | bytes 10485888 | tf_op jit(solution)/shard_map/ka,aij->kij/dot_general | solution.py:45
  277.3 3.8 copy.66
  281.1 2.8 copy.67
  283.8 7.6 %maximum_bitcast_fusion = f32[32,16,2,64,16]{3,4,0,1,2:T(8,128)} fusion(f32[16,1,64,32,16]{2,4,3,0,1:T(8,128)} %bitcast.78, f32[16,1,64,32,16]{2,4,3,0,1:T(8,128)} %bitcast.77), kind=kLoop, calls=%fused_computation.5 | loop fusion | flops 1048576 | bytes 8388608 | tf_op jit(solution)/shard_map/transpose | solution.py:110
  291.5 13.4 %copy.68 = f32[32,16,2,64,16]{0,4,3,2,1:T(8,128)} copy(f32[32,16,2,64,16]{3,4,0,1,2:T(8,128)} %maximum_bitcast_fusion) | data formatting | bytes 8388608 | tf_op jit(solution)/shard_map/transpose | solution.py:110
  304.8 11.7 %copy.69 = f32[32,16,2,1024]{3,1,2,0:T(8,128)} copy(f32[32,16,2,1024]{0,3,2,1:T(8,128)} %bitcast.74) | data formatting | bytes 8388608 | tf_op jit(solution)/shard_map/reshape | solution.py:113
  316.6 5.9 %all-to-all-start.1 = ((f32[32,16,2,1024]{3,1,2,0:T(8,128)}), f32[32,16,2,1024]{3,1,2,0:T(8,128)}, u32[]{:S(2)}, u32[]{:S(2)}) async-start(f32[32,16,2,1024]{3,1,2,0:T(8,128)} %copy.69), calls=%async_computation.1 | async-start | bytes 8388608 | tf_op jit(solution)/shard_map/all_to_all | solution.py:114
  322.5 0.1 broadcast_compare_fusion
  322.5 93.0 %all-to-all-done.1 = f32[32,16,2,1024]{3,1,2,0:T(8,128)} async-done(((f32[32,16,2,1024]{3,1,2,0:T(8,128)}), f32[32,16,2,1024]{3,1,2,0:T(8,128)}, u32[]{:S(2)}, u32[]{:S(2)}) %all-to-all-start.1) | async-done | bytes 4194336 | tf_op jit(solution)/shard_map/all_to_all | solution.py:114
  415.6 2.5 fusion.109
  418.1 3.0 fusion.6
  421.2 3.0 fusion.5
  424.2 3.0 fusion.23
  427.2 1.2 copy.72
  428.4 3.2 fusion.24
  431.7 1.2 copy.73
  432.9 2.5 fusion.4
  435.4 5.4 %copy.74 = f32[1024,2,512]{2,0,1:T(8,128)} copy(f32[1024,2,512]{0,2,1:T(8,128)} %fusion.4) | data formatting | bytes 8388608 | tf_op jit(solution)/shard_map/transpose | solution.py:126
  440.8 2.5 broadcast_select_fusion
  443.3 5.8 %copy.75 = f32[64,16,2,512]{3,2,1,0:T(2,128)} copy(f32[64,16,2,512]{3,1,0,2:T(8,128)S(1)} %broadcast_select_fusion) | data formatting | bytes 8388608 | tf_op jit(solution)/shard_map/jit(_where)/select_n | solution.py:130
  (7 shorter events, 0.1 us)
Async XLA Ops:
  6.5 230.6 %all-gather.2.cloned.1.call-start = ((), (), s32[]{:S(2)}) async-start(), calls=%async_computation.2 | async-start | bytes 9437184 | tf_op jit(solution)/shard_map/all_gather | solution.py:79
  237.1 5.8 %copy-start = (bf16[16,512,512]{2,1,0:T(8,128)(2,1)S(1)}, bf16[16,512,512]{2,1,0:T(8,128)(2,1)}, u32[]{:S(2)}) copy-start(bf16[16,512,512]{2,1,0:T(8,128)(2,1)} %all-gather.2.cloned.1.call-done) | copy-start | bytes 25165828
  242.9 1.2 copy-start.1
  316.6 99.0 %all-to-all-start.1 = ((f32[32,16,2,1024]{3,1,2,0:T(8,128)}), f32[32,16,2,1024]{3,1,2,0:T(8,128)}, u32[]{:S(2)}, u32[]{:S(2)}) async-start(f32[32,16,2,1024]{3,1,2,0:T(8,128)} %copy.69), calls=%async_computation.1 | async-start | bytes 8388608 | tf_op jit(solution)/shard_map/all_to_all | solution.py:114
Sparse Core Ops, SparseCore 0:
  65.6 171.4 all-gather.1
where the time goes:
time: 465 us; the launch traced here: 456 us
  waiting for transfers between devices  264 us (57%)
  local copies, waits for them, and re-layouts  65.8 us (14%)
  matrix products  45.3 us (10%)
  blocking collectives  36.5 us (8%)
  other arithmetic  25.2 us (5%)
  between operations  14 us (3%)
  starting transfers between devices  5.88 us (1%)
    all_gather x1, waiting for transfers between devices, shards(): piece = lax.all_gather(mine, 'inp', axis=1, tiled=True)  171 us
    all_to_all x1, waiting for transfers between devices, shards(): lax.all_to_all(arranged, 'chan', split_axis=0, concat_axis=0, tiled=True)  93 us
    all_to_all x1, blocking collectives, shards(): lax.all_to_all(spectra, 'chan', split_axis=3, concat_axis=1, tiled=True)  36.5 us
    dot_general x2, matrix products, complex_section(): jnp.einsum(form, sine, real_in, precision=highest)  20.4 us
    transpose x1, local copies, waits for them, and re-layouts, shards(): paired.reshape(chan_local, 2, input_rows, chan_count, col_local)  13.4 us
    reshape x1, local copies, waits for them, and re-layouts, shards(): arranged = arranged.reshape(chan_count, chan_local, 2, baseline_count)  11.7 us
  transfers between devices with their start and end apart: 2, of which 2 were waited for; matrix products, arithmetic and copies ran while one was open for 0% of the time, Pallas kernels for 0%

commit v1 on v0

v1 whole, which is shorter than its diff:
```python
import functools
import math

import jax
import jax.numpy as jnp
import ml_dtypes
import numpy as np
from jax import lax
from jax.experimental import pallas as pl
from jax.experimental.pallas import tpu as pltpu
from jax.sharding import PartitionSpec as P

NCH = 512
NSPEC = 256
LANES = 128
ALL = ("inp", "chan")


def taper_weights(count):
    position = np.arange(count, dtype=np.float64)
    return 0.5 - 0.5 * np.cos(2.0 * np.pi * (position + 0.5) / count)


def channel_tables():
    index = np.arange(NCH)
    angle = 2.0 * np.pi / NCH * (index[:, None] * index[None, :] % NCH)
    window = taper_weights(NCH)[None, :] / math.sqrt(NCH)
    cosine = (window * np.cos(angle)).astype(np.float32).astype(ml_dtypes.bfloat16)
    sine = (window * np.sin(angle)).astype(np.float32).astype(ml_dtypes.bfloat16)
    return cosine, sine


def delay_tables():
    channel = np.arange(NCH)
    half = NCH // 2
    angle = 2.0 * np.pi / NCH * (channel[:, None] * np.arange(half)[None, :] % NCH)
    weight = taper_weights(NCH)[:, None] * math.sqrt(NSPEC / NCH)
    both = np.concatenate([weight * np.cos(angle), weight * np.sin(angle)], axis=1)
    both = both.reshape(half, 2, NCH).transpose(1, 0, 2)
    return both.astype(np.float32).astype(ml_dtypes.bfloat16)


def channelize_kernel(volt_ref, cos_ref, sin_ref, out_ref, wide_ref, *, rows, spec_local):
    contract = (((1,), (1,)), ((), ()))
    for pair in range(spec_local // 2):
        plain, turned = [], []
        for spec in (2 * pair, 2 * pair + 1):
            real = volt_ref[0, :, spec * NCH : (spec + 1) * NCH]
            imag = volt_ref[1, :, spec * NCH : (spec + 1) * NCH]
            plain += [real, imag]
            turned += [imag, -real]
        plain = jnp.concatenate(plain, axis=0)
        turned = jnp.concatenate(turned, axis=0)
        out = lax.dot_general(cos_ref[...], plain, contract, preferred_element_type=jnp.float32)
        out += lax.dot_general(sin_ref[...], turned, contract, preferred_element_type=jnp.float32)
        for k in range(2):
            wide_ref[pl.ds(2 * pair + k, NCH, stride=spec_local), :] = out[:, k * LANES : (k + 1) * LANES]
    out_ref[...] = wide_ref[...].astype(jnp.bfloat16)


def correlate_kernel(spec_ref, out_ref, x_ref, scale_ref, *, blocks, times, rows):
    half = LANES // 2
    lane = lax.broadcasted_iota(jnp.int32, (rows, LANES), 1)
    row = lax.broadcasted_iota(jnp.int32, (rows, LANES), 0)
    sign = jnp.where(lane < half, 1.0, -1.0)
    diagonal = (lane % half) == row
    for ch in range(2):
        for block in range(blocks):
            part = spec_ref[block * times : (block + 1) * times, ch * 8 : (ch + 1) * 8, :]
            part = part.astype(jnp.float32).reshape(times * 8, LANES)
            x_ref[ch, :, block * LANES : (block + 1) * LANES] = part.astype(jnp.bfloat16)
            total = jnp.sum(part * part, axis=0, keepdims=True)
            total = total + pltpu.roll(total, half, axis=1)
            scale_ref[ch, block : block + 1, :] = lax.rsqrt(total / NSPEC + 1e-06)

    contract = (((0,), (0,)), ((), ()))
    for ch in range(2):
        for jblock in range(blocks):
            left = x_ref[ch, :, jblock * LANES : (jblock + 1) * LANES]
            product = lax.dot_general(left, x_ref[ch], contract, preferred_element_type=jnp.float32)
            row_scale = scale_ref[ch, jblock : jblock + 1, :]
            row_scale = jnp.transpose(jnp.broadcast_to(row_scale, (LANES, LANES)))[:rows] / NSPEC
            for iblock in range(blocks):
                first = product[:rows, iblock * LANES : (iblock + 1) * LANES]
                second = product[rows:, iblock * LANES : (iblock + 1) * LANES]
                value = first + sign * pltpu.roll(second, half, axis=1)
                value = value * (row_scale * scale_ref[ch, iblock : iblock + 1, :])
                if iblock == jblock:
                    value = jnp.where(diagonal, 0.0, value)
                value = value.astype(jnp.bfloat16)
                for a in range(4):
                    out_ref[iblock, jblock, a, ch] = value[a * 16 : (a + 1) * 16]


def delay_kernel(rho_ref, table_ref, out_ref, wide_ref, *, owners, rows, cols):
    half = NCH // 2
    wide_ref[...] = rho_ref[...].astype(jnp.float32)
    contract = (((0,), (0,)), ((), ()))
    group = 4
    for first in range(0, cols, group):
        parts = []
        for ch in range(2):
            left = [
                wide_ref[pl.ds(ch * cols + first + g, owners, stride=2 * cols), :].astype(jnp.bfloat16)
                for g in range(group)
            ]
            left = jnp.concatenate(left, axis=1)
            parts.append(
                lax.dot_general(left, table_ref[ch], contract, preferred_element_type=jnp.float32)
            )
        for g in range(group):
            sums = []
            for product in parts:
                real = product[g * LANES : g * LANES + rows]
                imag = product[g * LANES + rows : (g + 1) * LANES]
                sums.append((real[:, :half] + imag[:, half:], imag[:, :half] - real[:, half:]))
            even, odd = sums
            for part in range(2):
                low = even[part] + odd[part]
                high = even[part] - odd[part]
                for kb, value in enumerate((low[:, :LANES], low[:, LANES:], high[:, :LANES], high[:, LANES:])):
                    start = (first + g) * 8 + kb * 2 + part
                    out_ref[pl.ds(start, rows, stride=cols * 8), :] = value


def vmem(shape, dtype):
    return pltpu.VMEM(shape, dtype)


def shards(voltages):
    rows, _, local_time = voltages.shape
    chan_count = lax.axis_size("chan")
    inp_count = lax.axis_size("inp")
    owners = chan_count * inp_count
    spec_local = local_time // NCH
    cols = rows * inp_count // chan_count
    cosine, sine = channel_tables()
    slab = 2 * spec_local
    whole = pl.BlockSpec(memory_space=pltpu.VMEM)

    planes = voltages.transpose(1, 0, 2)
    spectra = pl.pallas_call(
        functools.partial(channelize_kernel, rows=rows, spec_local=spec_local),
        out_shape=jax.ShapeDtypeStruct((NCH * spec_local, LANES), jnp.bfloat16),
        in_specs=[whole] * 3,
        out_specs=whole,
        scratch_shapes=[vmem((NCH * spec_local, LANES), jnp.float32)],
        name="channelize",
    )(planes, jnp.asarray(cosine), jnp.asarray(sine))

    turned = lax.all_to_all(spectra.reshape(owners, slab, LANES), ALL, 0, 0, tiled=True)

    rho = pl.pallas_call(
        functools.partial(correlate_kernel, blocks=inp_count, times=chan_count, rows=rows),
        out_shape=jax.ShapeDtypeStruct((inp_count, inp_count, 4, 2, cols, LANES), jnp.bfloat16),
        in_specs=[whole],
        out_specs=whole,
        scratch_shapes=[
            vmem((2, NSPEC, inp_count * LANES), jnp.bfloat16),
            vmem((2, inp_count, LANES), jnp.float32),
        ],
        name="correlate",
    )(turned)

    rho = lax.all_to_all(rho.reshape(owners, 2 * cols, LANES), ALL, 0, 0, tiled=True)

    out = pl.pallas_call(
        functools.partial(delay_kernel, owners=owners, rows=rows, cols=cols),
        out_shape=jax.ShapeDtypeStruct((rows * cols * 8, LANES), jnp.float32),
        in_specs=[whole] * 2,
        out_specs=whole,
        scratch_shapes=[vmem((owners * 2 * cols, LANES), jnp.float32)],
        name="delay",
    )(rho.reshape(owners * 2 * cols, LANES), jnp.asarray(delay_tables()))
    out = out.reshape(rows, cols, NCH // LANES, 2, LANES).transpose(0, 1, 3, 2, 4)
    return out.reshape(rows, cols, 2, NCH)


def solution(mesh):
    return jax.shard_map(
        shards,
        mesh=mesh,
        in_specs=(P("inp", None, "chan"),),
        out_specs=P("inp", "chan", None, None),
        check_vma=False,
    )
```

time: 465 us -> 128 us (0.28); the launches traced: 456 us -> 128 us
  waiting for transfers between devices: 264 us -> 0 us
  blocking collectives: 36.5 us -> 107 us
  local copies, waits for them, and re-layouts: 65.8 us -> 2.77 us
  matrix products: 45.3 us -> 0 us
  other arithmetic: 25.2 us -> 0 us
  Pallas kernels: 0 us -> 18.2 us
  between operations: 14 us -> 0.01 us
  starting transfers between devices: 5.88 us -> 0 us
    all_gather x1 -> x0, waiting for transfers between devices: 171 us -> none  [shards(): piece = lax.all_gather(mine, 'inp', axis=1, tiled=True)]
    all_to_all x1 -> x0, waiting for transfers between devices: 93 us -> none  [shards(): lax.all_to_all(arranged, 'chan', split_axis=0, concat_axis=0, tiled=True)]
    all_to_all x1 -> x2, blocking collectives: 36.5 us -> 107 us  [the longest x1 60.3 us: shards(): lax.all_to_all(rho.reshape(owners, 2 * cols, LANES), ALL, 0, 0, tiled=True)]
    dot_general x11 -> x0, matrix products: 45.3 us -> none  [the longest x2 20.4 us: complex_section(): jnp.einsum(form, sine, real_in, precision=highest)]
    transpose x3 -> x0, local copies, waits for them, and re-layouts: 21.4 us -> none  [the longest x1 13.4 us: shards(): paired.reshape(chan_local, 2, input_rows, chan_count, col_local)]
    reshape x5 -> x0, local copies, waits for them, and re-layouts: 18.7 us -> none  [the longest x1 11.7 us: shards(): arranged = arranged.reshape(chan_count, chan_local, 2, baseline_count)]
    pallas_call x0 -> x3, Pallas kernels: none -> 18.2 us  [the longest x1 9.32 us: shards(): pl.pallas_call(functools.partial(delay_kernel, owners=owners, rows=rows,...]
    transpose x2 -> x0, other arithmetic: 10.1 us -> none  [the longest x1 7.63 us: shards(): paired.reshape(chan_local, 2, input_rows, chan_count, col_local)]
  transfers between devices with their start and end apart: 2 -> 0, of which waited for: 2 -> 0; matrix products, arithmetic and copies ran while one was open for 0% -> 0% of each run, Pallas kernels for 0% -> 0%
where the time goes in v1:
time: 128 us
  blocking collectives  107 us (84%)
  Pallas kernels  18.2 us (14%)
  local copies, waits for them, and re-layouts  2.77 us (2%)
    all_to_all x1, blocking collectives, shards(): lax.all_to_all(rho.reshape(owners, 2 * cols, LANES), ALL, 0, 0, tiled=True)  60.3 us
    all_to_all x1, blocking collectives, shards(): lax.all_to_all(spectra.reshape(owners, slab, LANES), ALL, 0, 0, tiled=True)  46.4 us
    pallas_call x1, Pallas kernels, shards(): pl.pallas_call(functools.partial(delay_kernel, owners=owners, rows=rows,...  9.32 us
    pallas_call x1, Pallas kernels, shards(): pl.pallas_call(functools.partial(correlate_kernel, blocks=inp_count, time...  4.91 us
    pallas_call x1, Pallas kernels, shards(): pl.pallas_call(functools.partial(channelize_kernel, rows=rows, spec_local...  3.95 us
    unnamed x1, local copies, waits for them, and re-layouts  2.77 us

profile of v1, /device:TPU:1, one launch (start us, length us, event | category | flops | bytes accessed | tf_op | source)
XLA Modules:
  0.0 127.7 jit_solution(14907200110202965891)
XLA Ops:
  0.0 2.8 %copy.8 = bf16[64,2,4096]{2,0,1:T(8,128)(2,1)} copy(bf16[64,2,4096]{2,1,0:T(2,128)(2,1)} %param.4) | data formatting | bytes 2097152 | tf_op args[0]
  2.8 4.0 %channelize.1 = bf16[4096,128]{1,0:T(8,128)(2,1)} custom-call(bf16[2,64,4096]{2,1,0:T(8,128)(2,1)} %bitcast.14, bf16[512,512]{1,0:T(8,128)(2,1)} %constant.6.clone.cos_ref, bf16[512,512]{1,0:T(8,128)(2,1)} %constant.7.clone.sin_ref), custom_call_target="tpu_custom_call" | custom-call | tf_op jit(solution)/shard_map/channelize/pallas_call | solution.py:142
  6.7 46.4 %all_to_all.10.spec_ref = bf16[256,16,128]{2,1,0:T(8,128)(2,1)} all-to-all(bf16[256,16,128]{2,1,0:T(8,128)(2,1)} %bitcast.13), channel_id=1, replica_groups=mesh['chan'=32,'inp'=8] {'inp','chan'}, dimensions={0} | all-to-all | bytes 2097152 | tf_op jit(solution)/shard_map/all_to_all | solution.py:151
  53.2 4.9 %correlate.1 = bf16[8,8,4,2,16,128]{5,4,3,2,1,0:T(8,128)(2,1)} custom-call(bf16[256,16,128]{2,1,0:T(8,128)(2,1)} %all_to_all.10.spec_ref), custom_call_target="tpu_custom_call" | custom-call | tf_op jit(solution)/shard_map/correlate/pallas_call | solution.py:153
  58.1 60.3 %all_to_all.11 = bf16[256,32,128]{2,1,0:T(8,128)(2,1)} all-to-all(bf16[256,32,128]{2,1,0:T(8,128)(2,1)} %bitcast.12), channel_id=1, replica_groups=mesh['chan'=32,'inp'=8] {'inp','chan'}, dimensions={0} | all-to-all | bytes 4194304 | tf_op jit(solution)/shard_map/all_to_all | solution.py:165
  118.4 9.3 %delay.1 = f32[8192,128]{1,0:T(8,128)} custom-call(bf16[8192,128]{1,0:T(8,128)(2,1)} %bitcast.11, bf16[2,256,512]{2,1,0:T(8,128)(2,1)} %constant.8.clone.table_ref), custom_call_target="tpu_custom_call" | custom-call | tf_op jit(solution)/shard_map/delay/pallas_call | solution.py:167

commit v2 on v1

v2 whole, which is shorter than its diff:
```python
import functools
import math

import jax
import jax.numpy as jnp
import ml_dtypes
import numpy as np
from jax import lax
from jax.experimental import pallas as pl
from jax.experimental.pallas import tpu as pltpu
from jax.sharding import PartitionSpec as P

NCH = 512
NSPEC = 256
LANES = 128
ALL = ("inp", "chan")


def taper_weights(count):
    position = np.arange(count, dtype=np.float64)
    return 0.5 - 0.5 * np.cos(2.0 * np.pi * (position + 0.5) / count)


def channel_tables():
    index = np.arange(NCH)
    angle = 2.0 * np.pi / NCH * (index[:, None] * index[None, :] % NCH)
    window = taper_weights(NCH)[None, :] / math.sqrt(NCH)
    cosine = (window * np.cos(angle)).astype(np.float32).astype(ml_dtypes.bfloat16)
    sine = (window * np.sin(angle)).astype(np.float32).astype(ml_dtypes.bfloat16)
    return cosine, sine


def delay_tables():
    channel = np.arange(NCH)
    half = NCH // 2
    angle = 2.0 * np.pi / NCH * (channel[:, None] * np.arange(half)[None, :] % NCH)
    weight = taper_weights(NCH)[:, None] * math.sqrt(NSPEC / NCH)
    both = np.concatenate([weight * np.cos(angle), weight * np.sin(angle)], axis=1)
    both = both.reshape(half, 2, NCH).transpose(1, 0, 2)
    return both.astype(np.float32).astype(ml_dtypes.bfloat16)


def channelize_kernel(volt_ref, cos_ref, sin_ref, out_ref, wide_ref, *, rows, spec_local):
    contract = (((1,), (1,)), ((), ()))
    for pair in range(spec_local // 2):
        plain, turned = [], []
        for spec in (2 * pair, 2 * pair + 1):
            real = volt_ref[0, :, spec * NCH : (spec + 1) * NCH]
            imag = volt_ref[1, :, spec * NCH : (spec + 1) * NCH]
            plain += [real, imag]
            turned += [imag, -real]
        plain = jnp.concatenate(plain, axis=0)
        turned = jnp.concatenate(turned, axis=0)
        out = lax.dot_general(cos_ref[...], plain, contract, preferred_element_type=jnp.float32)
        out += lax.dot_general(sin_ref[...], turned, contract, preferred_element_type=jnp.float32)
        for k in range(2):
            wide_ref[pl.ds(2 * pair + k, NCH, stride=spec_local), :] = out[:, k * LANES : (k + 1) * LANES]
    out_ref[...] = wide_ref[...].astype(jnp.bfloat16)


def correlate_kernel(
    spec_ref, out_ref, left_ref, right_ref, row_ref, col_ref, stage_ref, sems, *, blocks, times, rows
):
    half = LANES // 2
    lane = lax.broadcasted_iota(jnp.int32, (1, LANES), 1)
    sign = jnp.where(lane < half, 1.0, -1.0)
    for ch in range(2):
        for block in range(blocks):
            part = spec_ref[block * times : (block + 1) * times, ch * 8 : (ch + 1) * 8, :]
            part = part.astype(jnp.float32).reshape(times * 8, LANES)
            span = slice(block * LANES, (block + 1) * LANES)
            right_ref[ch, :NSPEC, span] = part.astype(jnp.bfloat16)
            right_ref[ch, NSPEC:, span] = (pltpu.roll(part, half, axis=1) * sign).astype(jnp.bfloat16)
            flipped = jnp.transpose(part.astype(jnp.bfloat16))
            left_ref[ch, block * rows : (block + 1) * rows, :NSPEC] = flipped[:rows]
            left_ref[ch, block * rows : (block + 1) * rows, NSPEC:] = flipped[rows:]
            total = jnp.sum(part * part, axis=0, keepdims=True)
            total = total + pltpu.roll(total, half, axis=1)
            scale = lax.rsqrt(total / NSPEC + 1e-06)
            col_ref[ch, block : block + 1, :] = scale
            scale = jnp.transpose(jnp.broadcast_to(scale, (LANES, LANES)))[:rows] / NSPEC
            row_ref[ch, block * rows : (block + 1) * rows, :] = scale

    diagonal = lax.broadcasted_iota(jnp.int32, (rows, LANES), 1) % half == lax.broadcasted_iota(
        jnp.int32, (rows, LANES), 0
    )
    copies = []
    for ch in range(2):
        for pair in range(blocks // 2):
            product = jnp.dot(
                left_ref[ch],
                right_ref[ch, :, pair * 2 * LANES : (pair + 1) * 2 * LANES],
                preferred_element_type=jnp.float32,
            )
            for iblock in (2 * pair, 2 * pair + 1):
                col = col_ref[ch, iblock : iblock + 1, :]
                for jblock in range(blocks):
                    span = slice(jblock * rows, (jblock + 1) * rows)
                    value = product[span, (iblock % 2) * LANES : (iblock % 2 + 1) * LANES]
                    value = value * (row_ref[ch, span, :] * col)
                    if iblock == jblock:
                        value = jnp.where(diagonal, 0.0, value)
                    value = value.astype(jnp.bfloat16)
                    for a in range(4):
                        stage_ref[ch, iblock, jblock, a] = value[a * 16 : (a + 1) * 16]
                copy = pltpu.make_async_copy(
                    stage_ref.at[ch, iblock], out_ref.at[iblock, :, :, ch], sems.at[ch, iblock]
                )
                copy.start()
                copies.append(copy)
    for copy in copies:
        copy.wait()


def delay_kernel(rho_ref, table_ref, out_ref, wide_ref, stage_ref, sems, *, owners, rows, cols):
    half = NCH // 2
    contract = (((0,), (0,)), ((), ()))
    group = 4
    sections = 2 * cols // 8
    flat_ref = stage_ref.reshape(cols * rows * 8, LANES)
    for section in range(sections):
        part = rho_ref[:, section * 8 : (section + 1) * 8, :].astype(jnp.float32)
        wide_ref[section] = part.reshape(owners * 8, LANES)
    copies = []
    for first in range(0, cols, group):
        parts = []
        for ch in range(2):
            left = []
            for g in range(group):
                row = ch * cols + first + g
                left.append(wide_ref[row // 8, pl.ds(row % 8, owners, stride=8), :].astype(jnp.bfloat16))
            left = jnp.concatenate(left, axis=1)
            parts.append(
                lax.dot_general(left, table_ref[ch], contract, preferred_element_type=jnp.float32)
            )
        for g in range(group):
            sums = []
            for product in parts:
                real = product[g * LANES : g * LANES + rows]
                imag = product[g * LANES + rows : (g + 1) * LANES]
                sums.append((real[:, :half] + imag[:, half:], imag[:, :half] - real[:, half:]))
            even, odd = sums
            for part in range(2):
                low = even[part] + odd[part]
                high = even[part] - odd[part]
                for kb, value in enumerate((low[:, :LANES], low[:, LANES:], high[:, :LANES], high[:, LANES:])):
                    start = (first + g) * rows * 8 + kb * 2 + part
                    flat_ref[pl.ds(start, rows, stride=8), :] = value
            copy = pltpu.make_async_copy(
                stage_ref.at[first + g], out_ref.at[:, first + g], sems.at[first + g]
            )
            copy.start()
            copies.append(copy)
    for copy in copies:
        copy.wait()


def fast(array):
    return pltpu.with_memory_space_constraint(array, pltpu.VMEM)


def shards(voltages):
    rows, _, local_time = voltages.shape
    chan_count = lax.axis_size("chan")
    inp_count = lax.axis_size("inp")
    owners = chan_count * inp_count
    spec_local = local_time // NCH
    cols = rows * inp_count // chan_count
    inputs = rows * inp_count
    cosine, sine = channel_tables()
    slab = 2 * spec_local
    whole = pl.BlockSpec(memory_space=pltpu.VMEM)

    planes = voltages.transpose(1, 0, 2)
    spectra = pl.pallas_call(
        functools.partial(channelize_kernel, rows=rows, spec_local=spec_local),
        out_shape=pltpu.VMEM((NCH * spec_local, LANES), jnp.bfloat16),
        in_specs=[whole] * 3,
        out_specs=whole,
        scratch_shapes=[pltpu.VMEM((NCH * spec_local, LANES), jnp.float32)],
        name="channelize",
    )(fast(planes), fast(jnp.asarray(cosine)), fast(jnp.asarray(sine)))

    turned = lax.all_to_all(spectra.reshape(owners, slab, LANES), ALL, 0, 0, tiled=True)

    rho = pl.pallas_call(
        functools.partial(correlate_kernel, blocks=inp_count, times=chan_count, rows=rows),
        out_shape=jax.ShapeDtypeStruct((inp_count, inp_count, 4, 2, cols, LANES), jnp.bfloat16),
        in_specs=[whole],
        out_specs=pl.BlockSpec(memory_space=pl.ANY),
        scratch_shapes=[
            pltpu.VMEM((2, inputs, 2 * NSPEC), jnp.bfloat16),
            pltpu.VMEM((2, 2 * NSPEC, 2 * inputs), jnp.bfloat16),
            pltpu.VMEM((2, inputs, LANES), jnp.float32),
            pltpu.VMEM((2, inp_count, LANES), jnp.float32),
            pltpu.VMEM((2, inp_count, inp_count, 4, cols, LANES), jnp.bfloat16),
            pltpu.SemaphoreType.DMA((2, inp_count)),
        ],
        name="correlate",
    )(fast(turned))

    rho = lax.all_to_all(rho.reshape(owners, 2 * cols, LANES), ALL, 0, 0, tiled=True)

    out = pl.pallas_call(
        functools.partial(delay_kernel, owners=owners, rows=rows, cols=cols),
        out_shape=jax.ShapeDtypeStruct((rows, cols, 8, LANES), jnp.float32),
        in_specs=[whole] * 2,
        out_specs=pl.BlockSpec(memory_space=pl.ANY),
        scratch_shapes=[
            pltpu.VMEM((2 * cols // 8, owners * 8, LANES), jnp.float32),
            pltpu.VMEM((cols, rows, 8, LANES), jnp.float32),
            pltpu.SemaphoreType.DMA((cols,)),
        ],
        name="delay",
    )(fast(rho), fast(jnp.asarray(delay_tables())))
    out = out.reshape(rows, cols, NCH // LANES, 2, LANES).transpose(0, 1, 3, 2, 4)
    return out.reshape(rows, cols, 2, NCH)


def solution(mesh):
    return jax.shard_map(
        shards,
        mesh=mesh,
        in_specs=(P("inp", None, "chan"),),
        out_specs=P("inp", "chan", None, None),
        check_vma=False,
    )
```

time: 128 us -> 116 us (0.906)
  Pallas kernels: 18.2 us -> 7.79 us
    pallas_call x1, Pallas kernels: 9.32 us -> 3.37 us  [shards(): pl.pallas_call(functools.partial(delay_kernel, owners=owners, rows=rows,...]
    pallas_call x1, Pallas kernels: 3.95 us -> 1.45 us  [shards(): pl.pallas_call(functools.partial(channelize_kernel, rows=rows, spec_local...]
    pallas_call x1, Pallas kernels: 4.91 us -> 2.98 us  [shards(): pl.pallas_call(functools.partial(correlate_kernel, blocks=inp_count, time...]
    unnamed x1 -> x7, local copies, waits for them, and re-layouts: 2.77 us -> 1.91 us
where the time goes in v2:
time: 116 us
  blocking collectives  106 us (91%)
  Pallas kernels  7.79 us (7%)
  local copies, waits for them, and re-layouts  1.91 us (2%)
    all_to_all x1, blocking collectives, shards(): lax.all_to_all(rho.reshape(owners, 2 * cols, LANES), ALL, 0, 0, tiled=True)  59.8 us
    all_to_all x1, blocking collectives, shards(): lax.all_to_all(spectra.reshape(owners, slab, LANES), ALL, 0, 0, tiled=True)  46.1 us
    pallas_call x1, Pallas kernels, shards(): pl.pallas_call(functools.partial(delay_kernel, owners=owners, rows=rows,...  3.37 us
    pallas_call x1, Pallas kernels, shards(): pl.pallas_call(functools.partial(correlate_kernel, blocks=inp_count, time...  2.98 us

profile of v2, /device:TPU:1, one launch (start us, length us, event | category | flops | bytes accessed | tf_op | source)
XLA Modules:
  0.0 115.7 jit_solution(1732391898983746414)
XLA Ops:
  0.0 0.0 copy-start
  0.0 0.0 copy-start.1
  0.0 1.9 %copy.8 = bf16[64,2,4096]{2,0,1:T(8,128)(2,1)S(1)} copy(bf16[64,2,4096]{2,1,0:T(2,128)(2,1)} %param.4) | data formatting | bytes 2097152 | tf_op args[0]
  1.9 0.0 copy-done
  1.9 0.0 copy-done.1
  1.9 1.5 %channelize.1 = bf16[4096,128]{1,0:T(8,128)(2,1)S(1)} custom-call(bf16[2,64,4096]{2,1,0:T(8,128)(2,1)S(1)} %bitcast.11, bf16[512,512]{1,0:T(8,128)(2,1)S(1)} %copy-done.1, bf16[512,512]{1,0:T(8,128)(2,1)S(1)} %copy-done), custom_call_target="tpu_custom_call" | custom-call | tf_op jit(solution)/shard_map/channelize/pallas_call | solution.py:175
  3.4 46.1 %all_to_all.10.spec_ref = bf16[256,16,128]{2,1,0:T(8,128)(2,1)S(1)} all-to-all(bf16[256,16,128]{2,1,0:T(8,128)(2,1)S(1)} %bitcast.10), channel_id=1, replica_groups=mesh['chan'=32,'inp'=8] {'inp','chan'}, dimensions={0} | all-to-all | bytes 2097152 | tf_op jit(solution)/shard_map/all_to_all | solution.py:184
  49.5 3.0 %correlate.1 = bf16[8,8,4,2,16,128]{5,4,3,2,1,0:T(8,128)(2,1)} custom-call(bf16[256,16,128]{2,1,0:T(8,128)(2,1)S(1)} %all_to_all.10.spec_ref), custom_call_target="tpu_custom_call" | custom-call | tf_op jit(solution)/shard_map/correlate/pallas_call | solution.py:186
  52.5 0.0 copy-start.2
  52.5 59.8 %all_to_all.11.rho_ref = bf16[256,32,128]{2,1,0:T(8,128)(2,1)S(1)} all-to-all(bf16[256,32,128]{2,1,0:T(8,128)(2,1)} %bitcast.12), channel_id=1, replica_groups=mesh['chan'=32,'inp'=8] {'inp','chan'}, dimensions={0} | all-to-all | bytes 4194304 | tf_op jit(solution)/shard_map/all_to_all | solution.py:202
  112.3 0.0 copy-done.2
  112.3 3.4 %delay.1 = f32[64,16,8,128]{3,2,1,0:T(8,128)} custom-call(bf16[256,32,128]{2,1,0:T(8,128)(2,1)S(1)} %all_to_all.11.rho_ref, bf16[2,256,512]{2,1,0:T(8,128)(2,1)S(1)} %copy-done.2), custom_call_target="tpu_custom_call" | custom-call | tf_op jit(solution)/shard_map/delay/pallas_call | solution.py:204
Async XLA Ops:
  0.0 1.9 %copy-start = (bf16[512,512]{1,0:T(8,128)(2,1)S(1)}, bf16[512,512]{1,0:T(8,128)(2,1)}, u32[]{:S(2)}) copy-start(bf16[512,512]{1,0:T(8,128)(2,1)} %constant.7.clone.sin_ref) | copy-start | bytes 1572868
  0.0 1.9 %copy-start.1 = (bf16[512,512]{1,0:T(8,128)(2,1)S(1)}, bf16[512,512]{1,0:T(8,128)(2,1)}, u32[]{:S(2)}) copy-start(bf16[512,512]{1,0:T(8,128)(2,1)} %constant.6.clone.cos_ref) | copy-start | bytes 1572868
  52.5 59.8 %copy-start.2 = (bf16[2,256,512]{2,1,0:T(8,128)(2,1)S(1)}, bf16[2,256,512]{2,1,0:T(8,128)(2,1)}, u32[]{:S(2)}) copy-start(bf16[2,256,512]{2,1,0:T(8,128)(2,1)} %constant.8.clone.table_ref) | copy-start | bytes 1572868

commit v3 on v2

v3 whole, which is shorter than its diff:
```python
import functools
import math

import jax
import jax.numpy as jnp
import ml_dtypes
import numpy as np
from jax import lax
from jax.experimental import pallas as pl
from jax.experimental.pallas import tpu as pltpu
from jax.sharding import PartitionSpec as P

NCH = 512
NSPEC = 256
LANES = 128
ALL = ("inp", "chan")


def taper_weights(count):
    position = np.arange(count, dtype=np.float64)
    return 0.5 - 0.5 * np.cos(2.0 * np.pi * (position + 0.5) / count)


def channel_tables():
    half = NCH // 2
    index = np.arange(NCH)
    angle = 2.0 * np.pi / NCH * (np.arange(half + 16)[:, None] * index[None, :] % NCH)
    window = taper_weights(NCH)[None, :] / math.sqrt(NCH)
    cosine = window * np.cos(angle)
    cosine[half + 1 :] = 0.0
    sine = (window * np.sin(angle))[:half]
    return tuple(part.astype(np.float32).astype(ml_dtypes.bfloat16) for part in (cosine, sine))


def delay_tables():
    half = NCH // 2
    owner = np.arange(half)
    channel = np.stack([owner, np.where(owner == 0, half, NCH - owner)])
    angle = 2.0 * np.pi / NCH * (channel[:, :, None] * np.arange(half) % NCH)
    weight = taper_weights(NCH)[channel][:, :, None] * math.sqrt(NSPEC / NCH)
    both = np.concatenate([weight * np.cos(angle), weight * np.sin(angle)], axis=2)
    both = both.reshape(2, half // 2, 2, NCH).transpose(2, 0, 1, 3).reshape(2, half, NCH)
    return both.astype(np.float32).astype(ml_dtypes.bfloat16)


def channelize_kernel(
    volt_hbm, cos_hbm, sin_hbm, out_ref, raw_ref, cos_ref, sin_ref, part_ref, wide_ref, sems, *, rows, specs
):
    half = NCH // 2
    tiles = NCH // LANES
    copies = [
        pltpu.make_async_copy(cos_hbm, cos_ref, sems.at[0]),
        pltpu.make_async_copy(sin_hbm, sin_ref, sems.at[1]),
    ]
    for spec in range(specs):
        copies.append(pltpu.make_async_copy(volt_hbm.at[:, spec], raw_ref.at[spec], sems.at[2 + spec]))
    for copy in (*copies[2:6], copies[0], copies[1], *copies[6:]):
        copy.start()

    def planes(spec):
        part_ref[spec] = raw_ref[spec].astype(jnp.float32).reshape(rows * 8, LANES)
        both = []
        for part in range(2):
            pieces = [part_ref[spec, pl.ds(2 * t + part, rows, stride=8), :] for t in range(tiles)]
            both.append(jnp.concatenate(pieces, axis=1).astype(jnp.bfloat16))
        return both

    contract = (((1,), (1,)), ((), ()))
    for pair in range(specs // 2):
        plain, turned = [], []
        if pair % 2 == 0:
            for copy in copies[2 + 2 * pair : 6 + 2 * pair]:
                copy.wait()
        for spec in (2 * pair, 2 * pair + 1):
            real, imag = planes(spec)
            plain += [real, imag]
            turned += [imag, -real]
        if pair == 0:
            copies[0].wait()
            copies[1].wait()
        even = lax.dot_general(
            cos_ref[...], jnp.concatenate(plain, axis=0), contract, preferred_element_type=jnp.float32
        )
        odd = lax.dot_general(
            sin_ref[...], jnp.concatenate(turned, axis=0), contract, preferred_element_type=jnp.float32
        )
        for k in range(2):
            spec = 2 * pair + k
            span = slice(k * LANES, (k + 1) * LANES)
            wide_ref[0, pl.ds(spec, half, stride=specs), :] = even[:half, span] + odd[:, span]
            wide_ref[1, pl.ds(spec, half, stride=specs), :] = even[:half, span] - odd[:, span]
            wide_ref[1, spec : spec + 1, :] = even[half : half + 1, span]
    first = wide_ref[0].reshape(half, specs, LANES)
    second = wide_ref[1].reshape(half, specs, LANES)
    out_ref[...] = jnp.concatenate([first, second], axis=1).astype(jnp.bfloat16)


def correlate_kernel(
    spec_ref, out_ref, left_ref, right_ref, row_ref, col_ref, stage_ref, sems, *, blocks, times, rows
):
    half = LANES // 2
    lane = lax.broadcasted_iota(jnp.int32, (1, LANES), 1)
    sign = jnp.where(lane < half, 1.0, -1.0)
    diagonal = lax.broadcasted_iota(jnp.int32, (rows, LANES), 1) % half == lax.broadcasted_iota(
        jnp.int32, (rows, LANES), 0
    )
    copies = []

    def prepare(ch, block):
        part = spec_ref[block * times : (block + 1) * times, ch * 8 : (ch + 1) * 8, :]
        part = part.astype(jnp.float32).reshape(times * 8, LANES)
        narrow = part.astype(jnp.bfloat16)
        span = slice(block * LANES, (block + 1) * LANES)
        right_ref[ch, :NSPEC, span] = narrow
        right_ref[ch, NSPEC:, span] = (pltpu.roll(part, half, axis=1) * sign).astype(jnp.bfloat16)
        flipped = jnp.transpose(narrow)
        left_ref[ch, block * rows : (block + 1) * rows, :NSPEC] = flipped[:rows]
        left_ref[ch, block * rows : (block + 1) * rows, NSPEC:] = flipped[rows:]
        total = jnp.sum(part * part, axis=0, keepdims=True)
        total = total + pltpu.roll(total, half, axis=1)
        scale = lax.rsqrt(total / NSPEC + 1e-06)
        col_ref[ch, block : block + 1, :] = scale
        scale = jnp.transpose(jnp.broadcast_to(scale, (LANES, LANES)))[:rows] / NSPEC
        row_ref[ch, block * rows : (block + 1) * rows, :] = scale

    def multiply(ch, pair):
        product = jnp.dot(
            left_ref[ch],
            right_ref[ch, :, pair * 2 * LANES : (pair + 1) * 2 * LANES],
            preferred_element_type=jnp.float32,
        )
        for iblock in (2 * pair, 2 * pair + 1):
            col = col_ref[ch, iblock : iblock + 1, :]
            for jblock in range(blocks):
                span = slice(jblock * rows, (jblock + 1) * rows)
                value = product[span, (iblock % 2) * LANES : (iblock % 2 + 1) * LANES]
                value = value * (row_ref[ch, span, :] * col)
                if iblock == jblock:
                    value = jnp.where(diagonal, 0.0, value)
                value = value.astype(jnp.bfloat16)
                for a in range(4):
                    stage_ref[ch, iblock, jblock, a] = value[a * 16 : (a + 1) * 16]
            copy = pltpu.make_async_copy(
                stage_ref.at[ch, iblock], out_ref.at[iblock, :, :, ch], sems.at[ch, iblock]
            )
            copy.start()
            copies.append(copy)

    for block in range(blocks):
        prepare(0, block)
    for pair in range(blocks // 2):
        multiply(0, pair)
        prepare(1, 2 * pair)
        prepare(1, 2 * pair + 1)
    for pair in range(blocks // 2):
        multiply(1, pair)
    for copy in copies:
        copy.wait()


def delay_kernel(rho_ref, table_ref, out_ref, wide_ref, stage_ref, sems, *, owners, rows, cols):
    half = NCH // 2
    contract = (((0,), (0,)), ((), ()))
    sections = 2 * cols // 8
    flat_ref = stage_ref.reshape(cols * rows * 8, LANES)
    copies = []

    def widen(section):
        part = rho_ref[:, section * 8 : (section + 1) * 8, :].astype(jnp.float32)
        part = part.reshape(owners // 2, 2, 8, LANES)
        for parity in range(2):
            wide_ref[section, parity] = part[:, parity].reshape(owners * 4, LANES)

    def transform(first, group):
        parts = []
        for parity in range(2):
            left = []
            for col in range(first, first + group):
                pieces = []
                for ch in range(2):
                    row = ch * cols + col
                    pieces.append(wide_ref[row // 8, parity, pl.ds(row % 8, owners // 2, stride=8), :])
                left.append(jnp.concatenate(pieces, axis=0).astype(jnp.bfloat16))
            left = jnp.concatenate(left, axis=1)
            parts.append(
                lax.dot_general(left, table_ref[parity], contract, preferred_element_type=jnp.float32)
            )
        for g in range(group):
            sums = []
            for product in parts:
                real = product[g * LANES : g * LANES + rows]
                imag = product[g * LANES + rows : (g + 1) * LANES]
                sums.append((real[:, :half] + imag[:, half:], imag[:, :half] - real[:, half:]))
            even, odd = sums
            for part in range(2):
                low = even[part] + odd[part]
                high = even[part] - odd[part]
                for kb, value in enumerate((low[:, :LANES], low[:, LANES:], high[:, :LANES], high[:, LANES:])):
                    start = (first + g) * rows * 8 + kb * 2 + part
                    flat_ref[pl.ds(start, rows, stride=8), :] = value
            copy = pltpu.make_async_copy(
                stage_ref.at[first + g], out_ref.at[:, first + g], sems.at[first + g]
            )
            copy.start()
            copies.append(copy)

    group = 4
    for first in range(0, cols, group):
        if first % 8 == 0:
            for ch in range(2):
                widen((ch * cols + first) // 8)
        transform(first, group)
    for copy in copies:
        copy.wait()


def fast(array):
    return pltpu.with_memory_space_constraint(array, pltpu.VMEM)


def shards(voltages):
    rows, _, local_time = voltages.shape
    chan_count = lax.axis_size("chan")
    inp_count = lax.axis_size("inp")
    owners = chan_count * inp_count
    spec_local = local_time // NCH
    cols = rows * inp_count // chan_count
    inputs = rows * inp_count
    cosine, sine = channel_tables()
    slab = 2 * spec_local
    tiles = NCH // LANES
    whole = pl.BlockSpec(memory_space=pltpu.VMEM)
    place = pl.BlockSpec(memory_space=pl.ANY)

    rowed = voltages.reshape(rows, 2, local_time // LANES, LANES).transpose(0, 2, 1, 3)
    rowed = rowed.reshape(rows, spec_local, 2 * tiles, LANES)
    spectra = pl.pallas_call(
        functools.partial(channelize_kernel, rows=rows, specs=spec_local),
        out_shape=pltpu.VMEM((owners, slab, LANES), jnp.bfloat16),
        in_specs=[place] * 3,
        out_specs=whole,
        scratch_shapes=[
            pltpu.VMEM((spec_local, rows, 2 * tiles, LANES), jnp.bfloat16),
            pltpu.VMEM(cosine.shape, jnp.bfloat16),
            pltpu.VMEM(sine.shape, jnp.bfloat16),
            pltpu.VMEM((spec_local, rows * 2 * tiles, LANES), jnp.float32),
            pltpu.VMEM((2, NCH // 2 * spec_local, LANES), jnp.float32),
            pltpu.SemaphoreType.DMA((2 + spec_local,)),
        ],
        name="channelize",
    )(rowed, jnp.asarray(cosine), jnp.asarray(sine))

    turned = lax.all_to_all(spectra, ALL, 0, 0, tiled=True)

    rho = pl.pallas_call(
        functools.partial(correlate_kernel, blocks=inp_count, times=chan_count, rows=rows),
        out_shape=jax.ShapeDtypeStruct((inp_count, inp_count, 4, 2, cols, LANES), jnp.bfloat16),
        in_specs=[whole],
        out_specs=place,
        scratch_shapes=[
            pltpu.VMEM((2, inputs, 2 * NSPEC), jnp.bfloat16),
            pltpu.VMEM((2, 2 * NSPEC, 2 * inputs), jnp.bfloat16),
            pltpu.VMEM((2, inputs, LANES), jnp.float32),
            pltpu.VMEM((2, inp_count, LANES), jnp.float32),
            pltpu.VMEM((2, inp_count, inp_count, 4, cols, LANES), jnp.bfloat16),
            pltpu.SemaphoreType.DMA((2, inp_count)),
        ],
        name="correlate",
    )(fast(turned))

    rho = lax.all_to_all(rho.reshape(owners, 2 * cols, LANES), ALL, 0, 0, tiled=True)

    out = pl.pallas_call(
        functools.partial(delay_kernel, owners=owners, rows=rows, cols=cols),
        out_shape=jax.ShapeDtypeStruct((rows, cols, 8, LANES), jnp.float32),
        in_specs=[whole] * 2,
        out_specs=place,
        scratch_shapes=[
            pltpu.VMEM((2 * cols // 8, 2, owners * 4, LANES), jnp.float32),
            pltpu.VMEM((cols, rows, 8, LANES), jnp.float32),
            pltpu.SemaphoreType.DMA((cols,)),
        ],
        name="delay",
    )(fast(rho), fast(jnp.asarray(delay_tables())))
    out = out.reshape(rows, cols, NCH // LANES, 2, LANES).transpose(0, 1, 3, 2, 4)
    return out.reshape(rows, cols, 2, NCH)


def solution(mesh):
    return jax.shard_map(
        shards,
        mesh=mesh,
        in_specs=(P("inp", None, "chan"),),
        out_specs=P("inp", "chan", None, None),
        check_vma=False,
    )
```

time: 116 us -> 115 us (level)
  local copies, waits for them, and re-layouts: 1.91 us -> 0.01 us
    unnamed x7 -> x2, local copies, waits for them, and re-layouts: 1.91 us -> 0.01 us
where the time goes in v3:
time: 115 us
  blocking collectives  106 us (92%)
  Pallas kernels  8.91 us (8%)
    all_to_all x1, blocking collectives, shards(): lax.all_to_all(rho.reshape(owners, 2 * cols, LANES), ALL, 0, 0, tiled=True)  59.8 us
    all_to_all x1, blocking collectives, shards(): turned = lax.all_to_all(spectra, ALL, 0, 0, tiled=True)  46.1 us
    pallas_call x1, Pallas kernels, shards(): pl.pallas_call(functools.partial(delay_kernel, owners=owners, rows=rows,...  3.37 us
    pallas_call x1, Pallas kernels, shards(): pl.pallas_call(functools.partial(correlate_kernel, blocks=inp_count, time...  2.99 us
    pallas_call x1, Pallas kernels, shards(): pl.pallas_call(functools.partial(channelize_kernel, rows=rows, specs=spec...  2.56 us

profile of v3, /device:TPU:1, one launch (start us, length us, event | category | flops | bytes accessed | tf_op | source)
XLA Modules:
  0.0 114.9 jit_solution(1510714002315530793)
XLA Ops:
  0.0 2.6 %channelize.1 = bf16[256,16,128]{2,1,0:T(8,128)(2,1)S(1)} custom-call(bf16[64,8,8,128]{3,2,1,0:T(8,128)(2,1)} %bitcast.12, bf16[272,512]{1,0:T(8,128)(2,1)} %constant.6.clone.cos_hbm, bf16[256,512]{1,0:T(8,128)(2,1)} %constant.7.clone.sin_hbm), custom_call_target="tpu_custom_call" | custom-call | tf_op jit(solution)/shard_map/channelize/pallas_call | solution.py:237
  2.6 46.1 %all_to_all.10.spec_ref = bf16[256,16,128]{2,1,0:T(8,128)(2,1)S(1)} all-to-all(bf16[256,16,128]{2,1,0:T(8,128)(2,1)S(1)} %channelize.1), channel_id=1, replica_groups=mesh['chan'=32,'inp'=8] {'inp','chan'}, dimensions={0} | all-to-all | bytes 2097152 | tf_op jit(solution)/shard_map/all_to_all | solution.py:253
  48.7 3.0 %correlate.1 = bf16[8,8,4,2,16,128]{5,4,3,2,1,0:T(8,128)(2,1)} custom-call(bf16[256,16,128]{2,1,0:T(8,128)(2,1)S(1)} %all_to_all.10.spec_ref), custom_call_target="tpu_custom_call" | custom-call | tf_op jit(solution)/shard_map/correlate/pallas_call | solution.py:255
  51.7 0.0 copy-start
  51.7 59.8 %all_to_all.11.rho_ref = bf16[256,32,128]{2,1,0:T(8,128)(2,1)S(1)} all-to-all(bf16[256,32,128]{2,1,0:T(8,128)(2,1)} %bitcast.11), channel_id=1, replica_groups=mesh['chan'=32,'inp'=8] {'inp','chan'}, dimensions={0} | all-to-all | bytes 4194304 | tf_op jit(solution)/shard_map/all_to_all | solution.py:271
  111.5 0.0 copy-done
  111.5 3.4 %delay.1 = f32[64,16,8,128]{3,2,1,0:T(8,128)} custom-call(bf16[256,32,128]{2,1,0:T(8,128)(2,1)S(1)} %all_to_all.11.rho_ref, bf16[2,256,512]{2,1,0:T(8,128)(2,1)S(1)} %copy-done), custom_call_target="tpu_custom_call" | custom-call | tf_op jit(solution)/shard_map/delay/pallas_call | solution.py:273
Async XLA Ops:
  51.7 59.8 %copy-start = (bf16[2,256,512]{2,1,0:T(8,128)(2,1)S(1)}, bf16[2,256,512]{2,1,0:T(8,128)(2,1)}, u32[]{:S(2)}) copy-start(bf16[2,256,512]{2,1,0:T(8,128)(2,1)} %constant.8.clone.table_ref) | copy-start | bytes 1572868

commit v4 on v3

--- a/solution.py
+++ b/solution.py
@@ -21,6 +21,11 @@
     return 0.5 - 0.5 * np.cos(2.0 * np.pi * (position + 0.5) / count)
 
 
+def by_lanes(table):
+    table = table.reshape(*table.shape[:-1], -1, LANES)
+    return np.moveaxis(table, -2, -3).astype(np.float32).astype(ml_dtypes.bfloat16)
+
+
 def channel_tables():
     half = NCH // 2
     index = np.arange(NCH)
@@ -29,7 +34,7 @@
     cosine = window * np.cos(angle)
     cosine[half + 1 :] = 0.0
     sine = (window * np.sin(angle))[:half]
-    return tuple(part.astype(np.float32).astype(ml_dtypes.bfloat16) for part in (cosine, sine))
+    return tuple(by_lanes(part) for part in (cosine, sine))
 
 
 def delay_tables():
@@ -38,9 +43,17 @@
     channel = np.stack([owner, np.where(owner == 0, half, NCH - owner)])
     angle = 2.0 * np.pi / NCH * (channel[:, :, None] * np.arange(half) % NCH)
     weight = taper_weights(NCH)[channel][:, :, None] * math.sqrt(NSPEC / NCH)
-    both = np.concatenate([weight * np.cos(angle), weight * np.sin(angle)], axis=2)
-    both = both.reshape(2, half // 2, 2, NCH).transpose(2, 0, 1, 3).reshape(2, half, NCH)
-    return both.astype(np.float32).astype(ml_dtypes.bfloat16)
+    cosine, sine = (
+        table.reshape(2, half // 2, 2, half).transpose(2, 0, 1, 3).reshape(2, half, half)
+        for table in (weight * np.cos(angle), weight * np.sin(angle))
+    )
+    upper = np.concatenate([cosine, -sine], axis=2)
+    lower = np.concatenate([sine, cosine], axis=2)
+    return by_lanes(np.concatenate([upper, lower], axis=1))
+
+
+def joined(blocks):
+    return jnp.concatenate([blocks[k] for k in range(blocks.shape[0])], axis=1)
 
 
 def channelize_kernel(
@@ -79,10 +92,10 @@
             copies[0].wait()
             copies[1].wait()
         even = lax.dot_general(
-            cos_ref[...], jnp.concatenate(plain, axis=0), contract, preferred_element_type=jnp.float32
+            joined(cos_ref), jnp.concatenate(plain, axis=0), contract, preferred_element_type=jnp.float32
         )
         odd = lax.dot_general(
-            sin_ref[...], jnp.concatenate(turned, axis=0), contract, preferred_element_type=jnp.float32
+            joined(sin_ref), jnp.concatenate(turned, axis=0), contract, preferred_element_type=jnp.float32
         )
         for k in range(2):
             spec = 2 * pair + k
@@ -108,25 +121,30 @@
 
     def prepare(ch, block):
         part = spec_ref[block * times : (block + 1) * times, ch * 8 : (ch + 1) * 8, :]
-        part = part.astype(jnp.float32).reshape(times * 8, LANES)
-        narrow = part.astype(jnp.bfloat16)
-        span = slice(block * LANES, (block + 1) * LANES)
-        right_ref[ch, :NSPEC, span] = narrow
-        right_ref[ch, NSPEC:, span] = (pltpu.roll(part, half, axis=1) * sign).astype(jnp.bfloat16)
+        wide = part.astype(jnp.float32).reshape(times * 8, LANES)
+        narrow = wide.astype(jnp.bfloat16)
+        right_ref[ch, block, :NSPEC] = narrow
+        right_ref[ch, block, NSPEC:] = (pltpu.roll(wide, half, axis=1) * sign).astype(jnp.bfloat16)
         flipped = jnp.transpose(narrow)
-        left_ref[ch, block * rows : (block + 1) * rows, :NSPEC] = flipped[:rows]
-        left_ref[ch, block * rows : (block + 1) * rows, NSPEC:] = flipped[rows:]
-        total = jnp.sum(part * part, axis=0, keepdims=True)
+        for part in range(2):
+            for k in range(NSPEC // LANES):
+                piece = flipped[part * rows : (part + 1) * rows, k * LANES : (k + 1) * LANES]
+                left_ref[ch, part * (NSPEC // LANES) + k, block * rows : (block + 1) * rows] = piece
+        total = jnp.sum(wide * wide, axis=0, keepdims=True)
         total = total + pltpu.roll(total, half, axis=1)
         scale = lax.rsqrt(total / NSPEC + 1e-06)
         col_ref[ch, block : block + 1, :] = scale
-        scale = jnp.transpose(jnp.broadcast_to(scale, (LANES, LANES)))[:rows] / NSPEC
-        row_ref[ch, block * rows : (block + 1) * rows, :] = scale
+
+    def spread(ch):
+        turned = jnp.transpose(col_ref[ch])[:rows] / NSPEC
+        for block in range(blocks):
+            column = jnp.broadcast_to(turned[:, block : block + 1], (rows, LANES))
+            row_ref[ch, block * rows : (block + 1) * rows, :] = column
 
     def multiply(ch, pair):
         product = jnp.dot(
-            left_ref[ch],
-            right_ref[ch, :, pair * 2 * LANES : (pair + 1) * 2 * LANES],
+            joined(left_ref.at[ch]),
+            joined(right_ref.at[ch, 2 * pair : 2 * pair + 2]),
             preferred_element_type=jnp.float32,
         )
         for iblock in (2 * pair, 2 * pair + 1):
@@ -148,10 +166,12 @@
 
     for block in range(blocks):
         prepare(0, block)
+    spread(0)
     for pair in range(blocks // 2):
         multiply(0, pair)
         prepare(1, 2 * pair)
         prepare(1, 2 * pair + 1)
+    spread(1)
     for pair in range(blocks // 2):
         multiply(1, pair)
     for copy in copies:
@@ -159,8 +179,6 @@
 
 
 def delay_kernel(rho_ref, table_ref, out_ref, wide_ref, stage_ref, sems, *, owners, rows, cols):
-    half = NCH // 2
-    contract = (((0,), (0,)), ((), ()))
     sections = 2 * cols // 8
     flat_ref = stage_ref.reshape(cols * rows * 8, LANES)
     copies = []
@@ -180,35 +198,29 @@
                 for ch in range(2):
                     row = ch * cols + col
                     pieces.append(wide_ref[row // 8, parity, pl.ds(row % 8, owners // 2, stride=8), :])
-                left.append(jnp.concatenate(pieces, axis=0).astype(jnp.bfloat16))
-            left = jnp.concatenate(left, axis=1)
-            parts.append(
-                lax.dot_general(left, table_ref[parity], contract, preferred_element_type=jnp.float32)
-            )
+                turned = jnp.transpose(jnp.concatenate(pieces, axis=0).astype(jnp.bfloat16))
+                left.append(jnp.concatenate([turned[:rows], turned[rows:]], axis=1))
+            left = jnp.concatenate(left, axis=0)
+            parts.append(jnp.dot(left, joined(table_ref.at[parity]), preferred_element_type=jnp.float32))
         for g in range(group):
-            sums = []
-            for product in parts:
-                real = product[g * LANES : g * LANES + rows]
-                imag = product[g * LANES + rows : (g + 1) * LANES]
-                sums.append((real[:, :half] + imag[:, half:], imag[:, :half] - real[:, half:]))
-            even, odd = sums
-            for part in range(2):
-                low = even[part] + odd[part]
-                high = even[part] - odd[part]
-                for kb, value in enumerate((low[:, :LANES], low[:, LANES:], high[:, :LANES], high[:, LANES:])):
+            even, odd = (product[g * rows : (g + 1) * rows] for product in parts)
+            for side, total in enumerate((even + odd, even - odd)):
+                for k in range(NCH // LANES):
+                    part, kb = k // 2, 2 * side + k % 2
                     start = (first + g) * rows * 8 + kb * 2 + part
-                    flat_ref[pl.ds(start, rows, stride=8), :] = value
+                    flat_ref[pl.ds(start, rows, stride=8), :] = total[:, k * LANES : (k + 1) * LANES]
             copy = pltpu.make_async_copy(
                 stage_ref.at[first + g], out_ref.at[:, first + g], sems.at[first + g]
             )
             copy.start()
             copies.append(copy)
 
-    group = 4
-    for first in range(0, cols, group):
-        if first % 8 == 0:
+    ready = 0
+    for first, group in ((0, 8), (8, 4), (12, 4)):
+        while ready < first + group:
             for ch in range(2):
-                widen((ch * cols + first) // 8)
+                widen((ch * cols + ready) // 8)
+            ready += 8
         transform(first, group)
     for copy in copies:
         copy.wait()
@@ -258,8 +270,8 @@
         in_specs=[whole],
         out_specs=place,
         scratch_shapes=[
-            pltpu.VMEM((2, inputs, 2 * NSPEC), jnp.bfloat16),
-            pltpu.VMEM((2, 2 * NSPEC, 2 * inputs), jnp.bfloat16),
+            pltpu.VMEM((2, 2 * NSPEC // LANES, inputs, LANES), jnp.bfloat16),
+            pltpu.VMEM((2, inp_count, 2 * NSPEC, LANES), jnp.bfloat16),
             pltpu.VMEM((2, inputs, LANES), jnp.float32),
             pltpu.VMEM((2, inp_count, LANES), jnp.float32),
             pltpu.VMEM((2, inp_count, inp_count, 4, cols, LANES), jnp.bfloat16),

time: 115 us -> 115 us (level)
  no operation moved by 1% of the time
where the time goes in v4:
time: 115 us
  blocking collectives  106 us (92%)
  Pallas kernels  8.74 us (8%)
    all_to_all x1, blocking collectives, shards(): lax.all_to_all(rho.reshape(owners, 2 * cols, LANES), ALL, 0, 0, tiled=True)  59.8 us
    all_to_all x1, blocking collectives, shards(): turned = lax.all_to_all(spectra, ALL, 0, 0, tiled=True)  46.1 us
    pallas_call x1, Pallas kernels, shards(): pl.pallas_call(functools.partial(delay_kernel, owners=owners, rows=rows,...  3.39 us
    pallas_call x1, Pallas kernels, shards(): pl.pallas_call(functools.partial(correlate_kernel, blocks=inp_count, time...  2.8 us
    pallas_call x1, Pallas kernels, shards(): pl.pallas_call(functools.partial(channelize_kernel, rows=rows, specs=spec...  2.56 us

profile of v4, /device:TPU:1, one launch (start us, length us, event | category | flops | bytes accessed | tf_op | source)
XLA Modules:
  0.0 114.7 jit_solution(3602894491663378645)
XLA Ops:
  0.0 2.6 %channelize.1 = bf16[256,16,128]{2,1,0:T(8,128)(2,1)S(1)} custom-call(bf16[64,8,8,128]{3,2,1,0:T(8,128)(2,1)} %bitcast.12, bf16[4,272,128]{2,1,0:T(8,128)(2,1)} %constant.6.clone.cos_hbm, bf16[4,256,128]{2,1,0:T(8,128)(2,1)} %constant.7.clone.sin_hbm), custom_call_target="tpu_custom_call" | custom-call | tf_op jit(solution)/shard_map/channelize/pallas_call | solution.py:249
  2.6 46.1 %all_to_all.10.spec_ref = bf16[256,16,128]{2,1,0:T(8,128)(2,1)S(1)} all-to-all(bf16[256,16,128]{2,1,0:T(8,128)(2,1)S(1)} %channelize.1), channel_id=1, replica_groups=mesh['chan'=32,'inp'=8] {'inp','chan'}, dimensions={0} | all-to-all | bytes 2097152 | tf_op jit(solution)/shard_map/all_to_all | solution.py:265
  48.7 2.8 %correlate.1 = bf16[8,8,4,2,16,128]{5,4,3,2,1,0:T(8,128)(2,1)} custom-call(bf16[256,16,128]{2,1,0:T(8,128)(2,1)S(1)} %all_to_all.10.spec_ref), custom_call_target="tpu_custom_call" | custom-call | tf_op jit(solution)/shard_map/correlate/pallas_call | solution.py:267
  51.5 0.0 copy-start
  51.5 59.8 %all_to_all.11.rho_ref = bf16[256,32,128]{2,1,0:T(8,128)(2,1)S(1)} all-to-all(bf16[256,32,128]{2,1,0:T(8,128)(2,1)} %bitcast.11), channel_id=1, replica_groups=mesh['chan'=32,'inp'=8] {'inp','chan'}, dimensions={0} | all-to-all | bytes 4194304 | tf_op jit(solution)/shard_map/all_to_all | solution.py:283
  111.3 0.0 copy-done
  111.3 3.4 %delay.1 = f32[64,16,8,128]{3,2,1,0:T(8,128)} custom-call(bf16[256,32,128]{2,1,0:T(8,128)(2,1)S(1)} %all_to_all.11.rho_ref, bf16[2,4,512,128]{3,2,1,0:T(8,128)(2,1)S(1)} %copy-done), custom_call_target="tpu_custom_call" | custom-call | tf_op jit(solution)/shard_map/delay/pallas_call | solution.py:285
Async XLA Ops:
  51.5 59.8 %copy-start = (bf16[2,4,512,128]{3,2,1,0:T(8,128)(2,1)S(1)}, bf16[2,4,512,128]{3,2,1,0:T(8,128)(2,1)}, u32[]{:S(2)}) copy-start(bf16[2,4,512,128]{3,2,1,0:T(8,128)(2,1)} %constant.8.clone.table_ref) | copy-start | bytes 3145732

commit v5 on v4

--- a/solution.py
+++ b/solution.py
@@ -109,7 +109,7 @@
 
 
 def correlate_kernel(
-    spec_ref, out_ref, left_ref, right_ref, row_ref, col_ref, stage_ref, sems, *, blocks, times, rows
+    spec_ref, out_ref, left_ref, right_ref, row_ref, col_ref, *, blocks, times, rows
 ):
     half = LANES // 2
     lane = lax.broadcasted_iota(jnp.int32, (1, LANES), 1)
@@ -117,7 +117,6 @@
     diagonal = lax.broadcasted_iota(jnp.int32, (rows, LANES), 1) % half == lax.broadcasted_iota(
         jnp.int32, (rows, LANES), 0
     )
-    copies = []
 
     def prepare(ch, block):
         part = spec_ref[block * times : (block + 1) * times, ch * 8 : (ch + 1) * 8, :]
@@ -157,12 +156,8 @@
                     value = jnp.where(diagonal, 0.0, value)
                 value = value.astype(jnp.bfloat16)
                 for a in range(4):
-                    stage_ref[ch, iblock, jblock, a] = value[a * 16 : (a + 1) * 16]
-            copy = pltpu.make_async_copy(
-                stage_ref.at[ch, iblock], out_ref.at[iblock, :, :, ch], sems.at[ch, iblock]
-            )
-            copy.start()
-            copies.append(copy)
+                    owner = (iblock * blocks + jblock) * 4 + a
+                    out_ref[owner, ch * 16 : (ch + 1) * 16] = value[a * 16 : (a + 1) * 16]
 
     for block in range(blocks):
         prepare(0, block)
@@ -174,17 +169,23 @@
     spread(1)
     for pair in range(blocks // 2):
         multiply(1, pair)
-    for copy in copies:
-        copy.wait()
-
-
-def delay_kernel(rho_ref, table_ref, out_ref, wide_ref, stage_ref, sems, *, owners, rows, cols):
+
+
+def delay_kernel(
+    rho_hbm, table_ref, out_ref, rho_ref, wide_ref, stage_ref, sems, arrive, *, owners, rows, cols
+):
     sections = 2 * cols // 8
     flat_ref = stage_ref.reshape(cols * rows * 8, LANES)
     copies = []
+    order = [ch * cols // 8 + k for k in range(cols // 8) for ch in range(2)]
+    fetches = {
+        k: pltpu.make_async_copy(rho_hbm.at[:, k * 8 : (k + 1) * 8], rho_ref.at[k], arrive.at[k]) for k in order
+    }
+    for k in order:
+        fetches[k].start()
 
     def widen(section):
-        part = rho_ref[:, section * 8 : (section + 1) * 8, :].astype(jnp.float32)
+        part = rho_ref[section].astype(jnp.float32)
         part = part.reshape(owners // 2, 2, 8, LANES)
         for parity in range(2):
             wide_ref[section, parity] = part[:, parity].reshape(owners * 4, LANES)
@@ -218,8 +219,11 @@
     ready = 0
     for first, group in ((0, 8), (8, 4), (12, 4)):
         while ready < first + group:
-            for ch in range(2):
-                widen((ch * cols + ready) // 8)
+            both = [(ch * cols + ready) // 8 for ch in range(2)]
+            for section in both:
+                fetches[section].wait()
+            for section in both:
+                widen(section)
             ready += 8
         transform(first, group)
     for copy in copies:
@@ -266,34 +270,34 @@
 
     rho = pl.pallas_call(
         functools.partial(correlate_kernel, blocks=inp_count, times=chan_count, rows=rows),
-        out_shape=jax.ShapeDtypeStruct((inp_count, inp_count, 4, 2, cols, LANES), jnp.bfloat16),
+        out_shape=pltpu.VMEM((owners, 2 * cols, LANES), jnp.bfloat16),
         in_specs=[whole],
-        out_specs=place,
+        out_specs=whole,
         scratch_shapes=[
             pltpu.VMEM((2, 2 * NSPEC // LANES, inputs, LANES), jnp.bfloat16),
             pltpu.VMEM((2, inp_count, 2 * NSPEC, LANES), jnp.bfloat16),
             pltpu.VMEM((2, inputs, LANES), jnp.float32),
             pltpu.VMEM((2, inp_count, LANES), jnp.float32),
-            pltpu.VMEM((2, inp_count, inp_count, 4, cols, LANES), jnp.bfloat16),
-            pltpu.SemaphoreType.DMA((2, inp_count)),
         ],
         name="correlate",
     )(fast(turned))
 
-    rho = lax.all_to_all(rho.reshape(owners, 2 * cols, LANES), ALL, 0, 0, tiled=True)
+    rho = lax.all_to_all(rho, ALL, 0, 0, tiled=True)
 
     out = pl.pallas_call(
         functools.partial(delay_kernel, owners=owners, rows=rows, cols=cols),
         out_shape=jax.ShapeDtypeStruct((rows, cols, 8, LANES), jnp.float32),
-        in_specs=[whole] * 2,
+        in_specs=[place, whole],
         out_specs=place,
         scratch_shapes=[
+            pltpu.VMEM((2 * cols // 8, owners, 8, LANES), jnp.bfloat16),
             pltpu.VMEM((2 * cols // 8, 2, owners * 4, LANES), jnp.float32),
             pltpu.VMEM((cols, rows, 8, LANES), jnp.float32),
             pltpu.SemaphoreType.DMA((cols,)),
+            pltpu.SemaphoreType.DMA((2 * cols // 8,)),
         ],
         name="delay",
-    )(fast(rho), fast(jnp.asarray(delay_tables())))
+    )(rho, fast(jnp.asarray(delay_tables())))
     out = out.reshape(rows, cols, NCH // LANES, 2, LANES).transpose(0, 1, 3, 2, 4)
     return out.reshape(rows, cols, 2, NCH)
 

time: 115 us -> 115 us (level)
    pallas_call x1, Pallas kernels: 3.39 us -> 4.81 us  [shards(): pl.pallas_call(functools.partial(delay_kernel, owners=owners, rows=rows,...]
    pallas_call x1, Pallas kernels: 2.8 us -> 1.63 us  [shards(): pl.pallas_call(functools.partial(correlate_kernel, blocks=inp_count, time...]
where the time goes in v5:
time: 115 us
  blocking collectives  106 us (92%)
  Pallas kernels  9 us (8%)
    all_to_all x1, blocking collectives, shards(): rho = lax.all_to_all(rho, ALL, 0, 0, tiled=True)  59.6 us
    all_to_all x1, blocking collectives, shards(): turned = lax.all_to_all(spectra, ALL, 0, 0, tiled=True)  46.1 us
    pallas_call x1, Pallas kernels, shards(): pl.pallas_call(functools.partial(delay_kernel, owners=owners, rows=rows,...  4.81 us
    pallas_call x1, Pallas kernels, shards(): pl.pallas_call(functools.partial(channelize_kernel, rows=rows, specs=spec...  2.56 us

profile of v5, /device:TPU:1, one launch (start us, length us, event | category | flops | bytes accessed | tf_op | source)
XLA Modules:
  0.0 114.7 jit_solution(205680286044427245)
XLA Ops:
  0.0 2.6 %channelize.1 = bf16[256,16,128]{2,1,0:T(8,128)(2,1)S(1)} custom-call(bf16[64,8,8,128]{3,2,1,0:T(8,128)(2,1)} %bitcast.10, bf16[4,272,128]{2,1,0:T(8,128)(2,1)} %constant.6.clone.cos_hbm, bf16[4,256,128]{2,1,0:T(8,128)(2,1)} %constant.7.clone.sin_hbm), custom_call_target="tpu_custom_call" | custom-call | tf_op jit(solution)/shard_map/channelize/pallas_call | solution.py:253
  2.6 46.1 %all_to_all.10.spec_ref = bf16[256,16,128]{2,1,0:T(8,128)(2,1)S(1)} all-to-all(bf16[256,16,128]{2,1,0:T(8,128)(2,1)S(1)} %channelize.1), channel_id=1, replica_groups=mesh['chan'=32,'inp'=8] {'inp','chan'}, dimensions={0} | all-to-all | bytes 2097152 | tf_op jit(solution)/shard_map/all_to_all | solution.py:269
  48.7 1.6 %correlate.1 = bf16[256,32,128]{2,1,0:T(8,128)(2,1)S(1)} custom-call(bf16[256,16,128]{2,1,0:T(8,128)(2,1)S(1)} %all_to_all.10.spec_ref), custom_call_target="tpu_custom_call" | custom-call | tf_op jit(solution)/shard_map/correlate/pallas_call | solution.py:271
  50.3 0.0 copy-start
  50.4 59.6 %all_to_all.11.rho_hbm = bf16[256,32,128]{2,1,0:T(8,128)(2,1)} all-to-all(bf16[256,32,128]{2,1,0:T(8,128)(2,1)S(1)} %correlate.1), channel_id=1, replica_groups=mesh['chan'=32,'inp'=8] {'inp','chan'}, dimensions={0} | all-to-all | bytes 4194304 | tf_op jit(solution)/shard_map/all_to_all | solution.py:285
  109.9 0.0 copy-done
  109.9 4.8 %delay.1 = f32[64,16,8,128]{3,2,1,0:T(8,128)} custom-call(bf16[256,32,128]{2,1,0:T(8,128)(2,1)} %all_to_all.11.rho_hbm, bf16[2,4,512,128]{3,2,1,0:T(8,128)(2,1)S(1)} %copy-done), custom_call_target="tpu_custom_call" | custom-call | tf_op jit(solution)/shard_map/delay/pallas_call | solution.py:287
Async XLA Ops:
  50.3 59.6 %copy-start = (bf16[2,4,512,128]{3,2,1,0:T(8,128)(2,1)S(1)}, bf16[2,4,512,128]{3,2,1,0:T(8,128)(2,1)}, u32[]{:S(2)}) copy-start(bf16[2,4,512,128]{3,2,1,0:T(8,128)(2,1)} %constant.8.clone.table_ref) | copy-start | bytes 3145732

commit v6 on v4

--- a/solution.py
+++ b/solution.py
@@ -13,6 +13,7 @@
 NCH = 512
 NSPEC = 256
 LANES = 128
+GROUPS = (4, 4, 4, 4)
 ALL = ("inp", "chan")
 
 
@@ -38,18 +39,19 @@
 
 
 def delay_tables():
-    half = NCH // 2
-    owner = np.arange(half)
-    channel = np.stack([owner, np.where(owner == 0, half, NCH - owner)])
-    angle = 2.0 * np.pi / NCH * (channel[:, :, None] * np.arange(half) % NCH)
-    weight = taper_weights(NCH)[channel][:, :, None] * math.sqrt(NSPEC / NCH)
-    cosine, sine = (
-        table.reshape(2, half // 2, 2, half).transpose(2, 0, 1, 3).reshape(2, half, half)
-        for table in (weight * np.cos(angle), weight * np.sin(angle))
-    )
-    upper = np.concatenate([cosine, -sine], axis=2)
-    lower = np.concatenate([sine, cosine], axis=2)
-    return by_lanes(np.concatenate([upper, lower], axis=1))
+    quarter = NCH // 4
+    tables = []
+    for kind in range(4):
+        channel = []
+        for ch, start in ((0, kind), (1, -kind % 4)):
+            owner = np.arange(start, NCH // 2, 4)
+            channel.append(owner if ch == 0 else np.where(owner == 0, NCH // 2, NCH - owner))
+        channel = np.concatenate(channel)
+        angle = 2.0 * np.pi / NCH * (channel[:, None] * np.arange(quarter) % NCH)
+        weight = taper_weights(NCH)[channel][:, None] * math.sqrt(NSPEC / NCH)
+        cosine, sine = weight * np.cos(angle), weight * np.sin(angle)
+        tables.append(np.block([[cosine, -sine], [sine, cosine]]))
+    return by_lanes(np.stack(tables))
 
 
 def joined(blocks):
@@ -67,7 +69,7 @@
     ]
     for spec in range(specs):
         copies.append(pltpu.make_async_copy(volt_hbm.at[:, spec], raw_ref.at[spec], sems.at[2 + spec]))
-    for copy in (*copies[2:6], copies[0], copies[1], *copies[6:]):
+    for copy in (*copies[2:4], copies[0], copies[1], *copies[4:]):
         copy.start()
 
     def planes(spec):
@@ -81,8 +83,8 @@
     contract = (((1,), (1,)), ((), ()))
     for pair in range(specs // 2):
         plain, turned = [], []
-        if pair % 2 == 0:
-            for copy in copies[2 + 2 * pair : 6 + 2 * pair]:
+        if pair < 2:
+            for copy in copies[4:] if pair else copies[2:4]:
                 copy.wait()
         for spec in (2 * pair, 2 * pair + 1):
             real, imag = planes(spec)
@@ -185,43 +187,56 @@
 
     def widen(section):
         part = rho_ref[:, section * 8 : (section + 1) * 8, :].astype(jnp.float32)
-        part = part.reshape(owners // 2, 2, 8, LANES)
-        for parity in range(2):
-            wide_ref[section, parity] = part[:, parity].reshape(owners * 4, LANES)
+        part = part.reshape(owners // 4, 4, 8, LANES)
+        for kind in range(4):
+            wide_ref[section, kind] = part[:, kind].reshape(owners * 2, LANES)
 
     def transform(first, group):
         parts = []
-        for parity in range(2):
+        for kind in range(4):
             left = []
             for col in range(first, first + group):
                 pieces = []
-                for ch in range(2):
+                for ch, source in ((0, kind), (1, -kind % 4)):
                     row = ch * cols + col
-                    pieces.append(wide_ref[row // 8, parity, pl.ds(row % 8, owners // 2, stride=8), :])
+                    pieces.append(wide_ref[row // 8, source, pl.ds(row % 8, owners // 4, stride=8), :])
                 turned = jnp.transpose(jnp.concatenate(pieces, axis=0).astype(jnp.bfloat16))
                 left.append(jnp.concatenate([turned[:rows], turned[rows:]], axis=1))
             left = jnp.concatenate(left, axis=0)
-            parts.append(jnp.dot(left, joined(table_ref.at[parity]), preferred_element_type=jnp.float32))
+            parts.append(jnp.dot(left, joined(table_ref.at[kind]), preferred_element_type=jnp.float32))
         for g in range(group):
-            even, odd = (product[g * rows : (g + 1) * rows] for product in parts)
-            for side, total in enumerate((even + odd, even - odd)):
-                for k in range(NCH // LANES):
-                    part, kb = k // 2, 2 * side + k % 2
+            zero, one, two, three = (
+                (product[g * rows : (g + 1) * rows, :LANES], product[g * rows : (g + 1) * rows, LANES:])
+                for product in parts
+            )
+            even, gap = [], []
+            for part in range(2):
+                even.append((zero[part] + two[part], one[part] + three[part]))
+                gap.append((zero[part] - two[part], one[part] - three[part]))
+            quarters = [
+                (even[0][0] + even[0][1], even[1][0] + even[1][1]),
+                (gap[0][0] + gap[1][1], gap[1][0] - gap[0][1]),
+                (even[0][0] - even[0][1], even[1][0] - even[1][1]),
+                (gap[0][0] - gap[1][1], gap[1][0] + gap[0][1]),
+            ]
+            for kb, pair in enumerate(quarters):
+                for part in range(2):
                     start = (first + g) * rows * 8 + kb * 2 + part
-                    flat_ref[pl.ds(start, rows, stride=8), :] = total[:, k * LANES : (k + 1) * LANES]
+                    flat_ref[pl.ds(start, rows, stride=8), :] = pair[part]
             copy = pltpu.make_async_copy(
                 stage_ref.at[first + g], out_ref.at[:, first + g], sems.at[first + g]
             )
             copy.start()
             copies.append(copy)
 
-    ready = 0
-    for first, group in ((0, 8), (8, 4), (12, 4)):
+    ready = first = 0
+    for group in GROUPS:
         while ready < first + group:
             for ch in range(2):
                 widen((ch * cols + ready) // 8)
             ready += 8
         transform(first, group)
+        first += group
     for copy in copies:
         copy.wait()
 
@@ -288,7 +303,7 @@
         in_specs=[whole] * 2,
         out_specs=place,
         scratch_shapes=[
-            pltpu.VMEM((2 * cols // 8, 2, owners * 4, LANES), jnp.float32),
+            pltpu.VMEM((2 * cols // 8, 4, owners * 2, LANES), jnp.float32),
             pltpu.VMEM((cols, rows, 8, LANES), jnp.float32),
             pltpu.SemaphoreType.DMA((cols,)),
         ],

time: 115 us -> 115 us (level)
  no operation moved by 1% of the time
where the time goes in v6:
time: 115 us; the launch traced here: 114 us
  blocking collectives  106 us (92%)
  Pallas kernels  8.48 us (7%)
    all_to_all x1, blocking collectives, shards(): lax.all_to_all(rho.reshape(owners, 2 * cols, LANES), ALL, 0, 0, tiled=True)  59.8 us
    all_to_all x1, blocking collectives, shards(): turned = lax.all_to_all(spectra, ALL, 0, 0, tiled=True)  46.1 us
    pallas_call x1, Pallas kernels, shards(): pl.pallas_call(functools.partial(delay_kernel, owners=owners, rows=rows,...  3.18 us
    pallas_call x1, Pallas kernels, shards(): pl.pallas_call(functools.partial(correlate_kernel, blocks=inp_count, time...  2.8 us
    pallas_call x1, Pallas kernels, shards(): pl.pallas_call(functools.partial(channelize_kernel, rows=rows, specs=spec...  2.5 us

profile of v6, /device:TPU:1, one launch (start us, length us, event | category | flops | bytes accessed | tf_op | source)
XLA Modules:
  0.0 114.4 jit_solution(18139008960029009058)
XLA Ops:
  0.0 2.5 %channelize.1 = bf16[256,16,128]{2,1,0:T(8,128)(2,1)S(1)} custom-call(bf16[64,8,8,128]{3,2,1,0:T(8,128)(2,1)} %bitcast.12, bf16[4,272,128]{2,1,0:T(8,128)(2,1)} %constant.6.clone.cos_hbm, bf16[4,256,128]{2,1,0:T(8,128)(2,1)} %constant.7.clone.sin_hbm), custom_call_target="tpu_custom_call" | custom-call | tf_op jit(solution)/shard_map/channelize/pallas_call | solution.py:264
  2.5 46.1 %all_to_all.10.spec_ref = bf16[256,16,128]{2,1,0:T(8,128)(2,1)S(1)} all-to-all(bf16[256,16,128]{2,1,0:T(8,128)(2,1)S(1)} %channelize.1), channel_id=1, replica_groups=mesh['chan'=32,'inp'=8] {'inp','chan'}, dimensions={0} | all-to-all | bytes 2097152 | tf_op jit(solution)/shard_map/all_to_all | solution.py:280
  48.6 2.8 %correlate.1 = bf16[8,8,4,2,16,128]{5,4,3,2,1,0:T(8,128)(2,1)} custom-call(bf16[256,16,128]{2,1,0:T(8,128)(2,1)S(1)} %all_to_all.10.spec_ref), custom_call_target="tpu_custom_call" | custom-call | tf_op jit(solution)/shard_map/correlate/pallas_call | solution.py:282
  51.5 0.0 copy-start
  51.5 59.8 %all_to_all.11.rho_ref = bf16[256,32,128]{2,1,0:T(8,128)(2,1)S(1)} all-to-all(bf16[256,32,128]{2,1,0:T(8,128)(2,1)} %bitcast.11), channel_id=1, replica_groups=mesh['chan'=32,'inp'=8] {'inp','chan'}, dimensions={0} | all-to-all | bytes 4194304 | tf_op jit(solution)/shard_map/all_to_all | solution.py:298
  111.3 0.0 copy-done
  111.3 3.2 %delay.1 = f32[64,16,8,128]{3,2,1,0:T(8,128)} custom-call(bf16[256,32,128]{2,1,0:T(8,128)(2,1)S(1)} %all_to_all.11.rho_ref, bf16[4,2,256,128]{3,2,1,0:T(8,128)(2,1)S(1)} %copy-done), custom_call_target="tpu_custom_call" | custom-call | tf_op jit(solution)/shard_map/delay/pallas_call | solution.py:300
Async XLA Ops:
  51.5 59.8 %copy-start = (bf16[4,2,256,128]{3,2,1,0:T(8,128)(2,1)S(1)}, bf16[4,2,256,128]{3,2,1,0:T(8,128)(2,1)}, u32[]{:S(2)}) copy-start(bf16[4,2,256,128]{3,2,1,0:T(8,128)(2,1)} %constant.8.clone.table_ref) | copy-start | bytes 1572868

commit v7 on v6

--- a/solution.py
+++ b/solution.py
@@ -13,7 +13,7 @@
 NCH = 512
 NSPEC = 256
 LANES = 128
-GROUPS = (4, 4, 4, 4)
+GROUPS = (8, 4, 2, 2)
 ALL = ("inp", "chan")
 
 
@@ -166,16 +166,12 @@
             copy.start()
             copies.append(copy)
 
-    for block in range(blocks):
-        prepare(0, block)
-    spread(0)
-    for pair in range(blocks // 2):
-        multiply(0, pair)
-        prepare(1, 2 * pair)
-        prepare(1, 2 * pair + 1)
-    spread(1)
-    for pair in range(blocks // 2):
-        multiply(1, pair)
+    for ch in range(2):
+        for block in range(blocks):
+            prepare(ch, block)
+        spread(ch)
+        for pair in range(blocks // 2):
+            multiply(ch, pair)
     for copy in copies:
         copy.wait()
 

time: 115 us -> 115 us (level)
  no operation moved by 1% of the time
where the time goes in v7:
time: 115 us; the launch traced here: 114 us
  blocking collectives  106 us (92%)
  Pallas kernels  8.44 us (7%)
    all_to_all x1, blocking collectives, shards(): lax.all_to_all(rho.reshape(owners, 2 * cols, LANES), ALL, 0, 0, tiled=True)  59.8 us
    all_to_all x1, blocking collectives, shards(): turned = lax.all_to_all(spectra, ALL, 0, 0, tiled=True)  46.1 us
    pallas_call x1, Pallas kernels, shards(): pl.pallas_call(functools.partial(delay_kernel, owners=owners, rows=rows,...  3.13 us
    pallas_call x1, Pallas kernels, shards(): pl.pallas_call(functools.partial(correlate_kernel, blocks=inp_count, time...  2.8 us
    pallas_call x1, Pallas kernels, shards(): pl.pallas_call(functools.partial(channelize_kernel, rows=rows, specs=spec...  2.5 us

profile of v7, /device:TPU:1, one launch (start us, length us, event | category | flops | bytes accessed | tf_op | source)
XLA Modules:
  0.0 114.4 jit_solution(2580735845183751122)
XLA Ops:
  0.0 2.5 %channelize.1 = bf16[256,16,128]{2,1,0:T(8,128)(2,1)S(1)} custom-call(bf16[64,8,8,128]{3,2,1,0:T(8,128)(2,1)} %bitcast.12, bf16[4,272,128]{2,1,0:T(8,128)(2,1)} %constant.6.clone.cos_hbm, bf16[4,256,128]{2,1,0:T(8,128)(2,1)} %constant.7.clone.sin_hbm), custom_call_target="tpu_custom_call" | custom-call | tf_op jit(solution)/shard_map/channelize/pallas_call | solution.py:260
  2.5 46.1 %all_to_all.10.spec_ref = bf16[256,16,128]{2,1,0:T(8,128)(2,1)S(1)} all-to-all(bf16[256,16,128]{2,1,0:T(8,128)(2,1)S(1)} %channelize.1), channel_id=1, replica_groups=mesh['chan'=32,'inp'=8] {'inp','chan'}, dimensions={0} | all-to-all | bytes 2097152 | tf_op jit(solution)/shard_map/all_to_all | solution.py:276
  48.6 2.8 %correlate.1 = bf16[8,8,4,2,16,128]{5,4,3,2,1,0:T(8,128)(2,1)} custom-call(bf16[256,16,128]{2,1,0:T(8,128)(2,1)S(1)} %all_to_all.10.spec_ref), custom_call_target="tpu_custom_call" | custom-call | tf_op jit(solution)/shard_map/correlate/pallas_call | solution.py:278
  51.5 0.0 copy-start
  51.5 59.8 %all_to_all.11.rho_ref = bf16[256,32,128]{2,1,0:T(8,128)(2,1)S(1)} all-to-all(bf16[256,32,128]{2,1,0:T(8,128)(2,1)} %bitcast.11), channel_id=1, replica_groups=mesh['chan'=32,'inp'=8] {'inp','chan'}, dimensions={0} | all-to-all | bytes 4194304 | tf_op jit(solution)/shard_map/all_to_all | solution.py:294
  111.3 0.0 copy-done
  111.3 3.1 %delay.1 = f32[64,16,8,128]{3,2,1,0:T(8,128)} custom-call(bf16[256,32,128]{2,1,0:T(8,128)(2,1)S(1)} %all_to_all.11.rho_ref, bf16[4,2,256,128]{3,2,1,0:T(8,128)(2,1)S(1)} %copy-done), custom_call_target="tpu_custom_call" | custom-call | tf_op jit(solution)/shard_map/delay/pallas_call | solution.py:296
Async XLA Ops:
  51.5 59.8 %copy-start = (bf16[4,2,256,128]{3,2,1,0:T(8,128)(2,1)S(1)}, bf16[4,2,256,128]{3,2,1,0:T(8,128)(2,1)}, u32[]{:S(2)}) copy-start(bf16[4,2,256,128]{3,2,1,0:T(8,128)(2,1)} %constant.8.clone.table_ref) | copy-start | bytes 1572868

commit v8 on v7

--- a/solution.py
+++ b/solution.py
@@ -83,8 +83,8 @@
     contract = (((1,), (1,)), ((), ()))
     for pair in range(specs // 2):
         plain, turned = [], []
-        if pair < 2:
-            for copy in copies[4:] if pair else copies[2:4]:
+        if pair < 3:
+            for copy in (copies[2:4], copies[4:6], copies[6:])[pair]:
                 copy.wait()
         for spec in (2 * pair, 2 * pair + 1):
             real, imag = planes(spec)

time: 115 us -> 115 us (level)
  no operation moved by 1% of the time
where the time goes in v8:
time: 115 us
  blocking collectives  106 us (92%)
  Pallas kernels  8.6 us (7%)
    all_to_all x1, blocking collectives, shards(): lax.all_to_all(rho.reshape(owners, 2 * cols, LANES), ALL, 0, 0, tiled=True)  59.8 us
    all_to_all x1, blocking collectives, shards(): turned = lax.all_to_all(spectra, ALL, 0, 0, tiled=True)  46.1 us
    pallas_call x1, Pallas kernels, shards(): pl.pallas_call(functools.partial(delay_kernel, owners=owners, rows=rows,...  3.14 us
    pallas_call x1, Pallas kernels, shards(): pl.pallas_call(functools.partial(correlate_kernel, blocks=inp_count, time...  2.8 us
    pallas_call x1, Pallas kernels, shards(): pl.pallas_call(functools.partial(channelize_kernel, rows=rows, specs=spec...  2.66 us

profile of v8, /device:TPU:1, one launch (start us, length us, event | category | flops | bytes accessed | tf_op | source)
XLA Modules:
  0.0 114.6 jit_solution(13058765274599047147)
XLA Ops:
  0.0 2.7 %channelize.1 = bf16[256,16,128]{2,1,0:T(8,128)(2,1)S(1)} custom-call(bf16[64,8,8,128]{3,2,1,0:T(8,128)(2,1)} %bitcast.12, bf16[4,272,128]{2,1,0:T(8,128)(2,1)} %constant.6.clone.cos_hbm, bf16[4,256,128]{2,1,0:T(8,128)(2,1)} %constant.7.clone.sin_hbm), custom_call_target="tpu_custom_call" | custom-call | tf_op jit(solution)/shard_map/channelize/pallas_call | solution.py:260
  2.7 46.1 %all_to_all.10.spec_ref = bf16[256,16,128]{2,1,0:T(8,128)(2,1)S(1)} all-to-all(bf16[256,16,128]{2,1,0:T(8,128)(2,1)S(1)} %channelize.1), channel_id=1, replica_groups=mesh['chan'=32,'inp'=8] {'inp','chan'}, dimensions={0} | all-to-all | bytes 2097152 | tf_op jit(solution)/shard_map/all_to_all | solution.py:276
  48.8 2.8 %correlate.1 = bf16[8,8,4,2,16,128]{5,4,3,2,1,0:T(8,128)(2,1)} custom-call(bf16[256,16,128]{2,1,0:T(8,128)(2,1)S(1)} %all_to_all.10.spec_ref), custom_call_target="tpu_custom_call" | custom-call | tf_op jit(solution)/shard_map/correlate/pallas_call | solution.py:278
  51.6 0.0 copy-start
  51.6 59.8 %all_to_all.11.rho_ref = bf16[256,32,128]{2,1,0:T(8,128)(2,1)S(1)} all-to-all(bf16[256,32,128]{2,1,0:T(8,128)(2,1)} %bitcast.11), channel_id=1, replica_groups=mesh['chan'=32,'inp'=8] {'inp','chan'}, dimensions={0} | all-to-all | bytes 4194304 | tf_op jit(solution)/shard_map/all_to_all | solution.py:294
  111.4 0.0 copy-done
  111.4 3.1 %delay.1 = f32[64,16,8,128]{3,2,1,0:T(8,128)} custom-call(bf16[256,32,128]{2,1,0:T(8,128)(2,1)S(1)} %all_to_all.11.rho_ref, bf16[4,2,256,128]{3,2,1,0:T(8,128)(2,1)S(1)} %copy-done), custom_call_target="tpu_custom_call" | custom-call | tf_op jit(solution)/shard_map/delay/pallas_call | solution.py:296
Async XLA Ops:
  51.6 59.8 %copy-start = (bf16[4,2,256,128]{3,2,1,0:T(8,128)(2,1)S(1)}, bf16[4,2,256,128]{3,2,1,0:T(8,128)(2,1)}, u32[]{:S(2)}) copy-start(bf16[4,2,256,128]{3,2,1,0:T(8,128)(2,1)} %constant.8.clone.table_ref) | copy-start | bytes 1572868
